TPU v7x, 256 devices: a whole 4x4x8 slice. The times are simulated.
256 devices in a mesh: walker: 16 (over x, y), tangent: 8 (over z), feat: 2 (over core).
Axes of the slice: x: 4, y: 4, z: 8, core: 2. Of those that a mesh axis runs over, the one named last changes fastest.
Arguments:
- value_in: bfloat16 [512, 512], P('walker', 'feat'), may hold values from -0.94921875 to 0.94921875
- tang_in: bfloat16 [512, 768, 512], P('walker', 'tangent', 'feat'), may hold values from -1.01 to 1.01
- lap_in: bfloat16 [512, 512], P('walker', 'feat'), may hold values from -6 to 6
- w_first: bfloat16 [512, 512], P(('walker', 'tangent', 'feat')), may hold values from -0.25 to 0.25
- b_first: float32 [512], replicated, may hold values from -3 to 3
- w_second: bfloat16 [512, 512], P(('walker', 'tangent', 'feat')), may hold values from -0.25 to 0.25
- b_second: float32 [512], replicated, may hold values from -3 to 3
- readout: float32 [512], replicated, may hold values from -0.6 to 0.6
Outputs:
- log_amplitude: float32 [512], P('walker')
- gradient: float32 [512, 768], P('walker', 'tangent')
- kinetic: float32 [512], P('walker')
All inputs are finite; a program needn't handle non-finite values.
Results may differ from a plain program's by a relative error of at most 0.0044.
Values may be sent and summed in bfloat16 or wider, within the bound.
No kernel may reach another device: no remote copies, remote signals or barrier semaphores. Data moves between devices by JAX's collectives and lax.ppermute only.
A program may use at most 64 MiB of HBM per device.

v0:
```python
import jax
import jax.numpy as jnp
from jax import lax
from jax.sharding import PartitionSpec as P


def tanh_layer(value, tangents, laplacian, w_full, bias):
    feat_index = lax.axis_index("feat")
    half_width = value.shape[1]
    count_w, count_t = (tangents.shape[0], tangents.shape[1])
    stacked = jnp.stack([value, laplacian])
    w_rows = lax.dynamic_slice_in_dim(w_full, feat_index * half_width, half_width, 0)
    partial_vl = jnp.einsum("kbd,de->kbe", stacked, w_rows, preferred_element_type=jnp.float32)
    partial_grad = jnp.dot(
        tangents.reshape(count_w * count_t, half_width), w_rows, preferred_element_type=jnp.float32
    ).reshape(count_w, count_t, w_full.shape[1])
    summed, grad_pre = (
        lax.psum_scatter(partial_vl, "feat", scatter_dimension=2, tiled=True),
        lax.psum_scatter(partial_grad, "feat", scatter_dimension=2, tiled=True),
    )
    pre_act = summed[0] + bias
    lap_pre = summed[1]
    hidden = jnp.tanh(pre_act)
    slope = 1.0 - hidden * hidden
    bend = -2.0 * hidden * slope
    return (hidden, slope, bend, grad_pre, lap_pre)


def own_half(vector, half_width):
    return lax.dynamic_slice_in_dim(vector, lax.axis_index("feat") * half_width, half_width, 0)


def per_device(value_in, tang_in, lap_in, w_first, b_first, w_second, b_second, readout):
    full_first, full_second = (
        lax.all_gather(w_first, ("walker", "tangent", "feat"), axis=0, tiled=True),
        lax.all_gather(w_second, ("walker", "tangent", "feat"), axis=0, tiled=True),
    )
    half_width = value_in.shape[1]
    value_start, lap_start, tangents_in = (value_in, lap_in, tang_in)
    bias_one = own_half(b_first, half_width)
    bias_two = own_half(b_second, half_width)
    read_weights = own_half(readout, half_width)
    hidden, slope, bend, grad_pre, lap_pre = tanh_layer(
        value_start, tangents_in, lap_start, full_first, bias_one
    )
    curv_first = lax.psum(jnp.sum(grad_pre * grad_pre, axis=1), "tangent")
    value_two = hidden.astype(jnp.bfloat16)
    tang_two = (slope[:, None, :] * grad_pre).astype(jnp.bfloat16)
    lap_two = (slope * lap_pre + bend * curv_first).astype(jnp.bfloat16)
    hidden, slope, bend, grad_pre, lap_pre = tanh_layer(
        value_two, tang_two, lap_two, full_second, bias_two
    )
    amp_part = jnp.sum(read_weights * hidden, axis=-1)
    grad_part = jnp.sum(grad_pre * (read_weights * slope)[:, None, :], axis=-1)
    local_squares = jnp.sum(grad_pre * grad_pre, axis=1)
    curv_second = lax.psum(local_squares, "tangent")
    lap_part = jnp.sum(read_weights * (slope * lap_pre + bend * curv_second), axis=-1)
    log_amplitude, gradient, laplace = lax.psum((amp_part, grad_part, lap_part), "feat")
    squares = lax.psum(jnp.sum(gradient * gradient, axis=-1), "tangent")
    kinetic = -0.5 * (laplace + squares)
    return (log_amplitude, gradient, kinetic)


def solution(mesh):
    placed = (
        P("walker", "feat"),
        P("walker", "tangent", "feat"),
        P("walker", "feat"),
        P(("walker", "tangent", "feat"), None),
        P(),
        P(("walker", "tangent", "feat"), None),
        P(),
        P(),
    )
    return jax.shard_map(
        per_device,
        mesh=mesh,
        in_specs=placed,
        out_specs=(P("walker"), P("walker", "tangent"), P("walker")),
        check_vma=False,
    )
```

profile of v0, /device:TPU:1, one launch (start us, length us, event | category | flops | bytes accessed | tf_op | source)
XLA Modules:
  0.0 270.8 jit_solution(8628064673603538799)
XLA Ops:
  7.2 0.0 copy-start
  7.2 0.0 reduce-scatter.5.cloned.1.call-start
  7.2 73.3 %all-gather = bf16[256,2,512]{2,1,0:T(2,128)(2,1)S(1)} all-gather(bf16[1,2,512]{2,1,0:T(2,128)(2,1)} %bitcast.67), channel_id=1, replica_groups=mesh['walker'=16,'tangent'=8,'feat'=2] {'walker','tangent','feat'}, dimensions={0}, use_global_device_ids=true | all-gather | bytes 526336 | tf_op jit(solution)/shard_map/all_gather | solution.py:35
  80.5 0.2 reshape.72
  80.7 1.6 fusion.5
  82.3 0.0 reduce-scatter.5.cloned.1.call-update
  82.3 0.0 reduce-scatter.7.cloned.1.call-start
  82.4 0.0 copy-done
  82.4 3.7 %convolution_bitcast_fusion = f32[3072,512]{0,1:T(8,128)} fusion(bf16[3072,256]{1,0:T(8,128)(2,1)S(1)} %bitcast.63, bf16[512,512]{1,0:T(8,128)(2,1)S(1)} %reshape.72, s32[]{:T(128)S(6)} %select_n.2), kind=kOutput, calls=%fused_computation | convolution fusion | flops 805306368 | bytes 8126468 | tf_op jit(solution)/shard_map/dot_general | solution.py:14
  86.1 6.6 %copy.13 = f32[3072,512]{1,0:T(8,128)} copy(f32[3072,512]{0,1:T(8,128)} %convolution_bitcast_fusion) | data formatting | bytes 12582912 | tf_op jit(solution)/shard_map/dot_general | solution.py:14
  92.7 0.0 copy-start.5
  92.7 0.0 copy-start.4
  92.7 0.0 reduce-scatter.7.cloned.1.call-update
  92.7 0.0 reduce-scatter.9.cloned.1.call-start
  92.8 0.6 copy-done.5
  93.4 0.1 dynamic_slice.17
  93.5 0.0 copy-done.4
  93.5 65.6 %all-gather.1 = bf16[256,2,512]{2,1,0:T(2,128)(2,1)S(1)} all-gather(bf16[1,2,512]{2,1,0:T(2,128)(2,1)S(1)} %bitcast.68), channel_id=1, replica_groups=mesh['walker'=16,'tangent'=8,'feat'=2] {'walker','tangent','feat'}, dimensions={0}, use_global_device_ids=true | all-gather | bytes 526336 | tf_op jit(solution)/shard_map/all_gather | solution.py:36
  159.1 0.2 reshape.74
  159.3 0.0 reduce-scatter.5.cloned.1.call-done
  159.3 0.0 copy-start.1
  159.3 0.8 tanh_convert_fusion
  160.2 0.0 reduce-scatter.7.cloned.1.call-done
  160.2 2.2 multiply_reduce_fusion.2
  162.4 22.1 %psum.42 = f32[32,256]{1,0:T(8,128)S(1)} all-reduce(f32[32,256]{1,0:T(8,128)S(1)} %multiply_reduce_fusion.2), channel_id=1, replica_groups=mesh['walker'=16,'tangent'=8,'feat'=2] {'tangent'}, use_global_device_ids=true, to_apply=%region_3.0 | all-reduce | flops 8192 | bytes 65536 | tf_op jit(solution)/shard_map/psum | solution.py:46
  184.6 0.0 copy-done.1
  184.6 0.8 fusion.3
  185.4 0.0 reduce-scatter.9.cloned.1.call-update
  185.4 0.0 reduce-scatter.11.cloned.1.call-start
  185.5 5.5 %fusion = f32[32,96,512]{2,1,0:T(8,128)} fusion(f32[32,96,256]{2,1,0:T(8,128)} %reduce-scatter.7.cloned.1.call-done, f32[32,256]{1,0:T(8,128)S(1)} %get-tuple-element.11, bf16[512,512]{1,0:T(8,128)(2,1)S(1)} %reshape.74, s32[]{:T(128)S(6)} %select_n.2), kind=kOutput, calls=%fused_computation.5 | convolution fusion | flops 806879232 | bytes 9732100 | tf_op jit(solution)/shard_map/dot_general | solution.py:14
  191.0 0.0 copy-start.6
  191.0 0.0 copy-start.7
  191.0 0.0 reduce-scatter.11.cloned.1.call-update
  191.1 0.7 copy-done.6
  191.7 0.1 dynamic_slice.15
  191.8 0.0 copy-done.7
  191.8 0.1 dynamic_slice.19
  191.9 9.7 %reduce-scatter.9.cloned.1.call-done = f32[2,32,256]{2,1,0:T(8,128)} async-done(((f32[2,32,512]{2,1,0:T(8,128)}), f32[2,32,256]{2,1,0:T(8,128)}) %reduce-scatter.9.cloned.1.call-update) | async-done | bytes 65552 | tf_op jit(solution)/shard_map/reduce_scatter | solution.py:18
  201.6 0.0 copy-start.2
  201.6 0.8 fusion.27
  202.4 21.9 %reduce-scatter.11.cloned.1.call-done = f32[32,96,256]{2,1,0:T(8,128)} async-done(((f32[32,96,512]{2,1,0:T(8,128)}), f32[32,96,256]{2,1,0:T(8,128)}) %reduce-scatter.11.cloned.1.call-update) | async-done | bytes 3145744 | tf_op jit(solution)/shard_map/reduce_scatter | solution.py:19
  224.4 2.5 multiply_reduce_fusion
  226.9 3.6 %psum.44 = f32[32,96]{1,0:T(8,128)S(1)} all-reduce(f32[32,96]{1,0:T(8,128)S(1)} %get-tuple-element.4), channel_id=1, replica_groups=mesh['walker'=16,'tangent'=8,'feat'=2] {'feat'}, use_global_device_ids=true, to_apply=%region_9.0 | all-reduce | flops 3072 | bytes 24576 | tf_op jit(solution)/shard_map/psum | solution.py:58
  230.5 0.0 copy-start.3
  230.5 0.1 multiply_reduce_fusion.4
  230.6 23.2 %all-reduce = (f32[32,256]{1,0:T(8,128)S(1)}, f32[32]{0:T(128)S(1)}) all-reduce(f32[32,256]{1,0:T(8,128)S(1)} %get-tuple-element.3, f32[32]{0:T(128)S(1)} %multiply_reduce_fusion.4), channel_id=1, replica_groups=mesh['walker'=16,'tangent'=8,'feat'=2] {'tangent'}, use_global_device_ids=true, to_apply=%region_11.0 | all-reduce | flops 8224 | bytes 65792 | tf_op jit(solution)/shard_map/psum | solution.py:56
  253.8 0.0 copy-done.2
  253.8 0.1 fusion.14
  253.9 9.9 %all-reduce.1 = (f32[32]{0:T(128)}, f32[32]{0:T(128)S(1)}) all-reduce(f32[32]{0:T(128)S(1)} %get-tuple-element.6, f32[32]{0:T(128)S(1)} %get-tuple-element.5), channel_id=1, replica_groups=mesh['walker'=16,'tangent'=8,'feat'=2] {'feat'}, use_global_device_ids=true, to_apply=%region_6.0 | all-reduce | flops 64 | bytes 512 | tf_op jit(solution)/shard_map/psum | solution.py:58
  263.8 0.5 add_multiply_fusion
  264.3 0.0 copy-done.3
  (1 shorter events, 0.0 us)
Async XLA Ops:
  7.2 75.2 %copy-start = (bf16[32,96,256]{2,1,0:T(8,128)(2,1)S(1)}, bf16[32,96,256]{2,1,0:T(8,128)(2,1)}, u32[]{:S(2)}) copy-start(bf16[32,96,256]{2,1,0:T(8,128)(2,1)} %param.9) | copy-start | bytes 4718596
  7.2 152.1 %reduce-scatter.5.cloned.1.call-start = ((), (), s32[]{:S(2)}) async-start(), calls=%async_computation.4 | async-start | bytes 196608 | tf_op jit(solution)/shard_map/reduce_scatter | solution.py:18
  82.3 77.9 %reduce-scatter.7.cloned.1.call-start = ((), (), s32[]{:S(2)}) async-start(), calls=%async_computation.5 | async-start | bytes 9437184 | tf_op jit(solution)/shard_map/reduce_scatter | solution.py:19
  92.7 0.7 copy-start.5
  92.7 0.8 copy-start.4
  92.7 108.9 %reduce-scatter.9.cloned.1.call-start = ((), (), s32[]{:S(2)}) async-start(), calls=%async_computation.6 | async-start | bytes 196608 | tf_op jit(solution)/shard_map/reduce_scatter | solution.py:18
  159.3 25.2 %copy-start.1 = (f32[2,32,256]{2,1,0:T(8,128)S(1)}, f32[2,32,256]{2,1,0:T(8,128)}, u32[]{:S(2)}) copy-start(f32[2,32,256]{2,1,0:T(8,128)} %reduce-scatter.5.cloned.1.call-done) | copy-start | bytes 196612
  185.4 38.9 %reduce-scatter.11.cloned.1.call-start = ((), (), s32[]{:S(2)}) async-start(), calls=%async_computation.7 | async-start | bytes 9437184 | tf_op jit(solution)/shard_map/reduce_scatter | solution.py:19
  191.0 0.7 copy-start.6
  191.0 0.8 copy-start.7
  201.6 52.2 %copy-start.2 = (f32[2,32,256]{2,1,0:T(8,128)S(1)}, f32[2,32,256]{2,1,0:T(8,128)}, u32[]{:S(2)}) copy-start(f32[2,32,256]{2,1,0:T(8,128)} %reduce-scatter.9.cloned.1.call-done) | copy-start | bytes 196612
  230.5 33.8 %copy-start.3 = (f32[32,96]{1,0:T(8,128)}, f32[32,96]{1,0:T(8,128)S(1)}, u32[]{:S(2)}) copy-start(f32[32,96]{1,0:T(8,128)S(1)} %psum.44) | copy-start | bytes 36868
Sparse Core Ops, SparseCore 0:
  82.5 9.7 reduce-scatter.4
  94.8 20.2 reduce-scatter.6
  185.6 15.9 reduce-scatter.8
  204.0 20.3 reduce-scatter.10
where the time goes:
time: 271 us
  blocking collectives  198 us (73%)
  waiting for transfers between devices  31.8 us (12%)
  between operations  13.9 us (5%)
  matrix products  11.6 us (4%)
  local copies, waits for them, and re-layouts  8.51 us (3%)
  other arithmetic  7.18 us (3%)
    all_gather x1, blocking collectives, per_device(): lax.all_gather(w_first, ('walker', 'tangent', 'feat'), axis=0, tiled=True)  73.3 us
    all_gather x1, blocking collectives, per_device(): lax.all_gather(w_second, ('walker', 'tangent', 'feat'), axis=0, tiled=True)  65.6 us
    psum x1, blocking collectives, per_device(): curv_second = lax.psum(local_squares, 'tangent')  23.2 us
    psum x1, blocking collectives, per_device(): curv_first = lax.psum(jnp.sum(grad_pre * grad_pre, axis=1), 'tangent')  22.1 us
    reduce_scatter x2, waiting for transfers between devices, tanh_layer(): lax.psum_scatter(partial_grad, 'feat', scatter_dimension=2, tiled=True)  21.9 us
    psum x2, blocking collectives, per_device(): lax.psum((amp_part, grad_part, lap_part), 'feat')  13.5 us
    reduce_scatter x2, waiting for transfers between devices, tanh_layer(): lax.psum_scatter(partial_vl, 'feat', scatter_dimension=2, tiled=True)  9.74 us
    dot_general x2, matrix products, tanh_layer(): jnp.dot(tangents.reshape(count_w * count_t, half_width), w_rows, preferre...  9.24 us
  transfers between devices with their start and end apart: 4, of which 2 were waited for; matrix products, arithmetic and copies ran while one was open for 7% of the time, Pallas kernels for 0%

commit v1 on v0

v1 whole, which is shorter than its diff:
```python
import jax
import jax.numpy as jnp
from jax import lax
from jax.experimental import pallas as pl
from jax.experimental.pallas import tpu as pltpu
from jax.sharding import PartitionSpec as P

BF16, F32 = jnp.bfloat16, jnp.float32
GROUP = 8
LANES = 128


def mm(a, b):
    return jnp.dot(a, b, preferred_element_type=F32)


class Halves:
    def __init__(self, c, half, w_own, w_oth, layer):
        self.index = (c, 1 - c)
        self.half = half
        self.weights = (w_own, w_oth)
        self.blocks = w_own.shape[0] // 2
        rows = w_own.shape[1] // 2
        self.rows = slice(layer * rows, (layer + 1) * rows)

    def block(self, k, j):
        w = self.weights[j][pl.ds(self.index[k] * self.blocks, self.blocks), self.rows, :]
        return w.reshape(self.half, self.half)

    def cols(self, j):
        return slice(j * self.half, (j + 1) * self.half)

    def vec(self, ref, j):
        return ref[:, pl.ds(pl.multiple_of(self.index[j] * self.half, self.half), self.half)]

    def apply(self, xs, j):
        return mm(xs[0], self.block(0, j)) + mm(xs[1], self.block(1, j))


def own_columns_kernel(t_own, t_oth, v_own, v_oth, l_own, l_oth, w_own, b1,
                       t2_own, aux):
    walkers = v_own.shape[0]
    mine, per, half = t2_own.shape
    c = lax.axis_index("feat")
    base = c * mine
    one = Halves(c, half, w_own, None, 0)
    vl = [jnp.concatenate([v[...], l[pl.ds(base, mine), :]], axis=0)
          for v, l in ((v_own, l_own), (v_oth, l_oth))]
    pre = one.apply(vl, 0)
    aux[:walkers, :] = jnp.tanh(pre[:walkers] + one.vec(b1, 0))
    aux[walkers:walkers + mine, :] = pre[walkers:]
    h1 = aux[pl.ds(base, mine), :]
    slope = 1.0 - h1 * h1
    for g in range(mine // GROUP):
        lo, hi = g * GROUP, (g + 1) * GROUP
        ts = [t[pl.ds(base + lo, GROUP)].reshape(GROUP * per, half) for t in (t_own, t_oth)]
        g1 = one.apply(ts, 0).reshape(GROUP, per, half)
        aux[walkers + mine + lo:walkers + mine + hi, :] = jnp.sum(g1 * g1, axis=1)
        t2_own[lo:hi] = (g1 * slope[lo:hi, None, :]).astype(BF16)


def rest_kernel(t_own, t_oth, t2_own, aux, v_own, v_oth, l_own, l_oth, w_own, w_oth, b1, b2, rd,
                amp_out, grad_out, s_out, h_sc, c1_sc, c2_sc):
    walkers = v_own.shape[0]
    mine, per, half = t2_own.shape
    c = lax.axis_index("feat")
    first_z = lax.axis_index("tangent") == 0
    base = c * mine
    one = Halves(c, half, w_own, w_oth, 0)
    two = Halves(c, half, w_own, w_oth, 1)
    vl = [jnp.concatenate([v[...], l[pl.ds(base, mine), :]], axis=0)
          for v, l in ((v_own, l_own), (v_oth, l_oth))]
    pre = one.apply(vl, 1)
    hid = jnp.tanh(pre[:walkers] + one.vec(b1, 1))
    h_sc[:walkers, one.cols(0)] = aux[:walkers, :]
    h_sc[:walkers, one.cols(1)] = hid
    lapin = [aux[walkers:walkers + mine, :], pre[walkers:]]
    value = [aux[:walkers, :].astype(BF16), hid.astype(BF16)]
    amp = None
    for j in (0, 1):
        hid = jnp.tanh(two.apply(value, j) + two.vec(b2, j))
        h_sc[walkers:, two.cols(j)] = hid
        term = two.vec(rd, j) * hid
        amp = term if amp is None else amp + term
    amp_out[...] = jnp.sum(amp[None], axis=-1)
    h1 = h_sc[pl.ds(base, mine), :]
    h2 = h_sc[pl.ds(walkers + base, mine), :]
    slope1 = 1.0 - h1 * h1
    slope2 = 1.0 - h2 * h2
    rs = [two.vec(rd, j) * slope2[:, two.cols(j)] for j in (0, 1)]
    for g in range(mine // GROUP):
        lo, hi = g * GROUP, (g + 1) * GROUP
        ts = [t[pl.ds(base + lo, GROUP)].reshape(GROUP * per, half) for t in (t_own, t_oth)]
        g1 = one.apply(ts, 1).reshape(GROUP, per, half)
        c1_sc[lo:hi, :] = jnp.sum(g1 * g1, axis=1)
        t2 = [t2_own[lo:hi].reshape(GROUP * per, half),
              (g1 * slope1[lo:hi, None, one.cols(1)]).astype(BF16).reshape(GROUP * per, half)]
        prod = None
        for j in (0, 1):
            g2 = two.apply(t2, j).reshape(GROUP, per, half)
            c2_sc[lo:hi, two.cols(j)] = jnp.sum(g2 * g2, axis=1)
            term = g2 * rs[j][lo:hi, None, :]
            prod = term if prod is None else prod + term
        grad_out[lo:hi, :] = jnp.sum(prod, axis=-1)
    curv = [aux[walkers + mine:, :], c1_sc[...]]
    laps = []
    for j in (0, 1):
        s1, h = slope1[:, one.cols(j)], h1[:, one.cols(j)]
        lap = jnp.where(first_z, s1 * lapin[j], 0.0) + (-2.0 * h * s1) * curv[j]
        high = lap.astype(BF16)
        laps.append(jnp.concatenate([high, (lap - high.astype(F32)).astype(BF16)], axis=0))
    total = None
    for j in (0, 1):
        both = two.apply(laps, j)
        h = h2[:, two.cols(j)]
        term = rs[j] * (both[:mine] + both[mine:] + (-2.0 * h) * c2_sc[:, two.cols(j)])
        total = term if total is None else total + term
    gr = grad_out[...]
    row = jnp.sum(total[None], axis=-1) + jnp.sum((gr * gr)[None], axis=-1)
    pair = jnp.concatenate([row, row], axis=1)
    lane = lax.broadcasted_iota(jnp.int32, pair.shape, 1)
    pair = jnp.where((lane >= base) & (lane < base + mine), pair, 0.0)
    s_out[...] = jnp.zeros_like(s_out)
    s_out[:, :walkers] = jnp.broadcast_to(pair, (s_out.shape[0], walkers))


def join_kernel(sums, grad, g_oth, amp, amp_out, grad_out, kin_out):
    mine = grad.shape[0]
    walkers = amp.shape[1]
    c = lax.axis_index("feat")
    amp_out[...] = amp[...]
    grad_out[pl.ds(c * mine, mine), :] = grad[...]
    grad_out[pl.ds((1 - c) * mine, mine), :] = g_oth[...]
    kin_out[...] = -0.5 * sums[:, :walkers]


def per_device(value_in, tang_in, lap_in, w_first, b_first, w_second, b_second, readout):
    walkers, half = value_in.shape
    per = tang_in.shape[1]
    n_z, n_c, n_w = lax.axis_size("tangent"), lax.axis_size("feat"), lax.axis_size("walker")
    mine = walkers // n_c
    peers = n_z * n_c
    rows = w_first.shape[0]
    swap = [(0, 1), (1, 0)]

    v_oth = lax.ppermute(value_in, "feat", swap)
    l_oth = lax.ppermute(lap_in, "feat", swap)
    t_oth = lax.ppermute(tang_in, "feat", swap)
    pair = jnp.concatenate([w_first, w_second], axis=0).reshape(2 * rows, n_c, half)
    piece = jnp.transpose(pair, (1, 0, 2))
    sent = jnp.broadcast_to(piece[None], (n_z, n_c, 2 * rows, half)).reshape(peers, 2 * rows, half)
    got = lax.all_to_all(sent, ("tangent", "feat"), 0, 0, tiled=True)
    got = jnp.transpose(got.reshape(peers, 2, rows, half), (1, 0, 2, 3)).reshape(2 * peers * rows, half)
    w_own = lax.all_to_all(jnp.broadcast_to(got[None], (n_w,) + got.shape), "walker", 0, 0, tiled=True)
    w_oth = lax.ppermute(w_own, "feat", swap)

    vm = pl.BlockSpec(memory_space=pltpu.VMEM)
    width = 2 * half
    params = pltpu.CompilerParams(vmem_limit_bytes=24 * 1024 * 1024)
    b1, b2, rd = b_first[None], b_second[None], readout[None]
    t2_own, aux = pl.pallas_call(
        own_columns_kernel,
        out_shape=(
            jax.ShapeDtypeStruct((mine, per, half), BF16),
            jax.ShapeDtypeStruct((walkers + 2 * mine, half), F32),
        ),
        in_specs=[vm] * 8,
        out_specs=(vm, vm),
        compiler_params=params,
        cost_estimate=pl.CostEstimate(flops=mine * per * width * width, bytes_accessed=1 << 22, transcendentals=0),
        name="own_columns",
    )(tang_in, t_oth, value_in, v_oth, lap_in, l_oth, w_own, b1)
    amp, grad, part = pl.pallas_call(
        rest_kernel,
        out_shape=(
            jax.ShapeDtypeStruct((1, walkers), F32),
            jax.ShapeDtypeStruct((mine, per), F32),
            jax.ShapeDtypeStruct((peers, LANES), F32),
        ),
        in_specs=[vm] * 13,
        out_specs=(vm, vm, vm),
        scratch_shapes=[
            pltpu.VMEM((2 * walkers, width), F32),
            pltpu.VMEM((mine, half), F32),
            pltpu.VMEM((mine, width), F32),
        ],
        compiler_params=params,
        cost_estimate=pl.CostEstimate(flops=3 * mine * per * width * width, bytes_accessed=1 << 22, transcendentals=0),
        name="rest",
    )(tang_in, t_oth, t2_own, aux, value_in, v_oth, lap_in, l_oth, w_own, w_oth, b1, b2, rd)

    g_oth = lax.ppermute(grad, "feat", swap)
    sums = lax.all_to_all(part.reshape(peers, 1, LANES), ("tangent", "feat"), 0, 0, tiled=True)
    total = jnp.sum(sums, axis=0)
    amp, gradient, kinetic = pl.pallas_call(
        join_kernel,
        out_shape=(
            jax.ShapeDtypeStruct((1, walkers), F32),
            jax.ShapeDtypeStruct((walkers, per), F32),
            jax.ShapeDtypeStruct((1, walkers), F32),
        ),
        in_specs=[vm] * 4,
        out_specs=(vm, vm, vm),
        compiler_params=pltpu.CompilerParams(vmem_limit_bytes=2 * 1024 * 1024),
        name="join",
    )(total, grad, g_oth, amp)
    return amp.reshape(walkers), gradient, kinetic.reshape(walkers)


def solution(mesh):
    placed = (
        P("walker", "feat"),
        P("walker", "tangent", "feat"),
        P("walker", "feat"),
        P(("walker", "tangent", "feat"), None),
        P(),
        P(("walker", "tangent", "feat"), None),
        P(),
        P(),
    )

    return jax.shard_map(
        per_device,
        mesh=mesh,
        in_specs=placed,
        out_specs=(P("walker"), P("walker", "tangent"), P("walker")),
        check_vma=False,
    )
```

time: 271 us -> 54.5 us (0.20)
  blocking collectives: 198 us -> 31 us
  waiting for transfers between devices: 31.8 us -> 7.78 us
  between operations: 13.9 us -> 0.73 us
  matrix products: 11.6 us -> 0 us
  starting transfers between devices: 0.16 us -> 9.81 us
  local copies, waits for them, and re-layouts: 8.51 us -> 0.17 us
  other arithmetic: 7.18 us -> 0.74 us
  Pallas kernels: 0 us -> 3.97 us
    all_gather x2 -> x0, blocking collectives: 139 us -> none  [the longest x1 73.3 us: per_device(): lax.all_gather(w_first, ('walker', 'tangent', 'feat'), axis=0, tiled=True)]
    psum x4 -> x0, blocking collectives: 58.8 us -> none  [the longest x1 23.2 us: per_device(): curv_second = lax.psum(local_squares, 'tangent')]
    reduce_scatter x4 -> x0, waiting for transfers between devices: 31.7 us -> none  [the longest x2 21.9 us: tanh_layer(): lax.psum_scatter(partial_grad, 'feat', scatter_dimension=2, tiled=True)]
    all_to_all x0 -> x2, blocking collectives: none -> 31 us  [the longest x1 16.9 us: per_device(): lax.all_to_all(jnp.broadcast_to(got[None], (n_w,) + got.shape), 'walker',...]
    dot_general x4 -> x0, matrix products: 11.6 us -> none  [the longest x2 9.24 us: tanh_layer(): jnp.dot(tangents.reshape(count_w * count_t, half_width), w_rows, preferre...]
    all_to_all x0 -> x1, waiting for transfers between devices: none -> 6.7 us  [per_device(): lax.all_to_all(part.reshape(peers, 1, LANES), ('tangent', 'feat'), 0, 0,...]
    dot_general x1 -> x0, local copies, waits for them, and re-layouts: 6.61 us -> none  [tanh_layer(): jnp.dot(tangents.reshape(count_w * count_t, half_width), w_rows, preferre...]
    ppermute x0 -> x5, starting transfers between devices: none -> 6.17 us  [the longest x1 3.29 us: per_device(): t_oth = lax.ppermute(tang_in, 'feat', swap)]
  transfers between devices with their start and end apart: 4 -> 6, of which waited for: 2 -> 2; matrix products, arithmetic and copies ran while one was open for 7% -> 2% of each run, Pallas kernels for 0% -> 1%
where the time goes in v1:
time: 54.5 us; the launch traced here: 54.2 us
  blocking collectives  31 us (57%)
  starting transfers between devices  9.81 us (18%)
  waiting for transfers between devices  7.78 us (14%)
  Pallas kernels  3.97 us (7%)
  other arithmetic  0.74 us (1%)
  between operations  0.73 us (1%)
    all_to_all x1, blocking collectives, per_device(): lax.all_to_all(jnp.broadcast_to(got[None], (n_w,) + got.shape), 'walker',...  16.9 us
    all_to_all x1, blocking collectives, per_device(): got = lax.all_to_all(sent, ('tangent', 'feat'), 0, 0, tiled=True)  14.1 us
    all_to_all x1, waiting for transfers between devices, per_device(): lax.all_to_all(part.reshape(peers, 1, LANES), ('tangent', 'feat'), 0, 0,...  6.7 us
    all_to_all x1, starting transfers between devices, per_device(): lax.all_to_all(part.reshape(peers, 1, LANES), ('tangent', 'feat'), 0, 0,...  3.64 us
    ppermute x1, starting transfers between devices, per_device(): t_oth = lax.ppermute(tang_in, 'feat', swap)  3.29 us
    pallas_call x1, Pallas kernels, per_device(): pl.pallas_call(rest_kernel, out_shape=(jax.ShapeDtypeStruct((1, walkers),...  2.71 us
    ppermute x1, starting transfers between devices, per_device(): w_oth = lax.ppermute(w_own, 'feat', swap)  2.07 us
  transfers between devices with their start and end apart: 6, of which 2 were waited for; matrix products, arithmetic and copies ran while one was open for 2% of the time, Pallas kernels for 1%

profile of v1, /device:TPU:1, one launch (start us, length us, event | category | flops | bytes accessed | tf_op | source)
XLA Modules:
  0.0 54.2 jit_solution(17417337162206639688)
XLA Ops:
  0.6 0.0 copy-start
  0.6 0.0 copy-start.1
  0.7 0.0 copy-start.2
  0.7 0.0 copy-start.3
  0.7 3.3 %collective-permute-start = (bf16[32,96,256]{2,1,0:T(8,128)(2,1)}, bf16[32,96,256]{2,1,0:T(8,128)(2,1)S(1)}, u32[]{:S(2)}, u32[]{:S(2)}) collective-permute-start(bf16[32,96,256]{2,1,0:T(8,128)(2,1)} %t_own.3), channel_id=1, source_target_pairs={{0,1},{1,0},{2,3},{3,2},{4,5},{5,4},{6,7},{7,6},{8,9},{9,8},{10,11... | collective-permute-start | bytes 4718600 | tf_op jit(solution)/shard_map/ppermute | solution.py:148
  4.0 0.7 %pad_maximum_fusion = bf16[4,512]{1,0:T(4,128)(2,1)S(1)} fusion(bf16[2,512]{1,0:T(2,128)(2,1)} %param.13, bf16[2,512]{1,0:T(2,128)(2,1)} %param.11), kind=kLoop, calls=%fused_computation | loop fusion | flops 8192 | bytes 8192 | tf_op jit(solution)/shard_map/concatenate | solution.py:149
  4.7 14.1 %all_to_all.15 = bf16[16,4,256]{2,1,0:T(4,128)(2,1)S(1)} all-to-all(bf16[16,4,256]{2,1,0:T(4,128)(2,1)S(1)} %bitcast.19), channel_id=1, replica_groups=mesh['walker'=16,'tangent'=8,'feat'=2] {'tangent','feat'}, dimensions={0} | all-to-all | bytes 65536 | tf_op jit(solution)/shard_map/all_to_all | solution.py:152
  18.9 16.9 %all_to_all.16.w_own = bf16[16,64,256]{2,1,0:T(8,128)(2,1)S(1)} all-to-all(bf16[16,64,256]{2,1,0:T(8,128)(2,1)S(1)} %broadcast_in_dim.24), channel_id=1, replica_groups=mesh['walker'=16,'tangent'=8,'feat'=2] {'walker'}, dimensions={0} | all-to-all | bytes 1048576 | tf_op jit(solution)/shard_map/all_to_all | solution.py:154
  35.8 2.1 %collective-permute-start.3 = (bf16[16,64,256]{2,1,0:T(8,128)(2,1)S(1)}, bf16[16,64,256]{2,1,0:T(8,128)(2,1)S(1)}, u32[]{:S(2)}, u32[]{:S(2)}) collective-permute-start(bf16[16,64,256]{2,1,0:T(8,128)(2,1)S(1)} %all_to_all.16.w_own), channel_id=1, source_target_pairs={{0,1},{1,0},{2,3},{3,2},{4,5},{5,4},{6,7},{7,6},{8,9},{9,8},{10,11... | collective-permute-start | bytes 1572872 | tf_op jit(solution)/shard_map/ppermute | solution.py:155
  37.9 0.0 copy-done.1
  37.9 0.0 collective-permute-start.1
  37.9 0.0 copy-done.2
  37.9 0.5 collective-permute-start.2
  38.4 1.0 %collective-permute-done.1.v_oth = bf16[32,256]{1,0:T(8,128)(2,1)S(1)} collective-permute-done((bf16[32,256]{1,0:T(8,128)(2,1)S(1)}, bf16[32,256]{1,0:T(8,128)(2,1)S(1)}, u32[]{:S(2)}, u32[]{:S(2)}) %collective-permute-start.1) | collective-permute-done | bytes 16416 | tf_op jit(solution)/shard_map/ppermute | solution.py:146
  39.5 0.0 collective-permute-done.2.l_oth
  39.5 0.0 collective-permute-done.t_oth
  39.5 0.0 copy-done
  39.5 0.0 copy-done.3
  39.5 0.0 copy-start.4
  39.5 0.0 copy-start.5
  39.5 0.6 %own_columns.1 = (bf16[16,96,256]{2,1,0:T(8,128)(2,1)S(1)}, f32[64,256]{1,0:T(8,128)S(1)}) custom-call(bf16[32,96,256]{2,1,0:T(8,128)(2,1)S(1)} %copy-done, bf16[32,96,256]{2,1,0:T(8,128)(2,1)S(1)} %collective-permute-done.t_oth, bf16[32,256]{1,0:T(8,128)(2,1)S(1)} %copy-done.1, bf16[32,256]{1,0:T(8,128)(2,1)S(1)} %collective-permute-done.1.v_oth, ...), custom_call_target="tpu_custom_call" | custom-call | flops 402653184 | bytes 4194304 | tf_op jit(solution)/shard_map/own_columns/pallas_call | solution.py:161
  40.2 0.0 collective-permute-done.3.w_oth
  40.2 0.0 copy-done.4
  40.2 0.0 copy-done.5
  40.2 2.7 %rest.1 = (f32[1,32]{1,0:T(1,128)S(1)}, f32[16,96]{1,0:T(8,128)S(1)}, f32[16,128]{1,0:T(8,128)}) custom-call(bf16[32,96,256]{2,1,0:T(8,128)(2,1)S(1)} %copy-done, bf16[32,96,256]{2,1,0:T(8,128)(2,1)S(1)} %collective-permute-done.t_oth, bf16[16,96,256]{2,1,0:T(8,128)(2,1)S(1)} %get-tuple-element.11.t2_own, f32[64,256]{1,0:T(8,128)S(1)} %get-tuple-element.12.aux, ...), custom_call_target="tpu_custom_call" | custom-call | flops 1207959552 | bytes 4194304 | tf_op jit(solution)/shard_map/rest/pallas_call | solution.py:173
  42.9 3.6 %all-to-all-start.2 = ((f32[16,1,128]{2,1,0:T(1,128)}), f32[16,1,128]{2,1,0:T(1,128)S(1)}, u32[]{:S(2)}, u32[]{:S(2)}) async-start(f32[16,1,128]{2,1,0:T(1,128)} %bitcast.8), calls=%async_computation.2 | async-start | bytes 16384 | tf_op jit(solution)/shard_map/all_to_all | solution.py:193
  46.5 0.3 collective-permute-start.4
  46.8 6.7 %all-to-all-done.2 = f32[16,1,128]{2,1,0:T(1,128)S(1)} async-done(((f32[16,1,128]{2,1,0:T(1,128)}), f32[16,1,128]{2,1,0:T(1,128)S(1)}, u32[]{:S(2)}, u32[]{:S(2)}) %all-to-all-start.2) | async-done | bytes 8224 | tf_op jit(solution)/shard_map/all_to_all | solution.py:193
  53.6 0.0 collective-permute-done.4.g_oth
  53.6 0.6 %join.1 = (f32[1,32]{1,0:T(1,128)}, f32[32,96]{1,0:T(8,128)}, f32[1,32]{1,0:T(1,128)}) custom-call(f32[1,128]{1,0:T(1,128)S(1)} %bitcast.18, f32[16,96]{1,0:T(8,128)S(1)} %get-tuple-element.14.grad, f32[16,96]{1,0:T(8,128)S(1)} %collective-permute-done.4.g_oth, f32[1,32]{1,0:T(1,128)S(1)} %get-tuple-element.15.amp), custom_call_target="tpu_custom_call" | custom-call | tf_op jit(solution)/shard_map/join/pallas_call | solution.py:195
  (8 shorter events, 0.2 us)
Async XLA Ops:
  0.6 38.9 %copy-start = (bf16[32,96,256]{2,1,0:T(8,128)(2,1)S(1)}, bf16[32,96,256]{2,1,0:T(8,128)(2,1)}, u32[]{:S(2)}) copy-start(bf16[32,96,256]{2,1,0:T(8,128)(2,1)} %t_own.3) | copy-start | bytes 4718596
  0.6 37.3 %copy-start.1 = (bf16[32,256]{1,0:T(8,128)(2,1)S(1)}, bf16[32,256]{1,0:T(8,128)(2,1)}, u32[]{:S(2)}) copy-start(bf16[32,256]{1,0:T(8,128)(2,1)} %v_own.3) | copy-start | bytes 49156
  0.7 37.2 %copy-start.2 = (bf16[32,256]{1,0:T(8,128)(2,1)S(1)}, bf16[32,256]{1,0:T(8,128)(2,1)}, u32[]{:S(2)}) copy-start(bf16[32,256]{1,0:T(8,128)(2,1)} %l_own.3) | copy-start | bytes 49156
  0.7 38.8 %copy-start.3 = (f32[512]{0:T(512)S(1)}, f32[512]{0:T(512)}, u32[]{:S(2)}) copy-start(f32[512]{0:T(512)} %param.12) | copy-start | bytes 6148
  0.7 38.8 %collective-permute-start = (bf16[32,96,256]{2,1,0:T(8,128)(2,1)}, bf16[32,96,256]{2,1,0:T(8,128)(2,1)S(1)}, u32[]{:S(2)}, u32[]{:S(2)}) collective-permute-start(bf16[32,96,256]{2,1,0:T(8,128)(2,1)} %t_own.3), channel_id=1, source_target_pairs={{0,1},{1,0},{2,3},{3,2},{4,5},{5,4},{6,7},{7,6},{8,9},{9,8},{10,11... | collective-permute-start | bytes 4718600 | tf_op jit(solution)/shard_map/ppermute | solution.py:148
  35.8 4.3 %collective-permute-start.3 = (bf16[16,64,256]{2,1,0:T(8,128)(2,1)S(1)}, bf16[16,64,256]{2,1,0:T(8,128)(2,1)S(1)}, u32[]{:S(2)}, u32[]{:S(2)}) collective-permute-start(bf16[16,64,256]{2,1,0:T(8,128)(2,1)S(1)} %all_to_all.16.w_own), channel_id=1, source_target_pairs={{0,1},{1,0},{2,3},{3,2},{4,5},{5,4},{6,7},{7,6},{8,9},{9,8},{10,11... | collective-permute-start | bytes 1572872 | tf_op jit(solution)/shard_map/ppermute | solution.py:155
  37.9 1.6 %collective-permute-start.1 = (bf16[32,256]{1,0:T(8,128)(2,1)S(1)}, bf16[32,256]{1,0:T(8,128)(2,1)S(1)}, u32[]{:S(2)}, u32[]{:S(2)}) collective-permute-start(bf16[32,256]{1,0:T(8,128)(2,1)S(1)} %copy-done.1), channel_id=1, source_target_pairs={{0,1},{1,0},{2,3},{3,2},{4,5},{5,4},{6,7},{7,6},{8,9},{9,8},{10,11... | collective-permute-start | bytes 49160 | tf_op jit(solution)/shard_map/ppermute | solution.py:146
  37.9 1.6 %collective-permute-start.2 = (bf16[32,256]{1,0:T(8,128)(2,1)S(1)}, bf16[32,256]{1,0:T(8,128)(2,1)S(1)}, u32[]{:S(2)}, u32[]{:S(2)}) collective-permute-start(bf16[32,256]{1,0:T(8,128)(2,1)S(1)} %copy-done.2), channel_id=1, source_target_pairs={{0,1},{1,0},{2,3},{3,2},{4,5},{5,4},{6,7},{7,6},{8,9},{9,8},{10,11... | collective-permute-start | bytes 49160 | tf_op jit(solution)/shard_map/ppermute | solution.py:147
  39.5 0.7 %copy-start.4 = (f32[512]{0:T(512)S(1)}, f32[512]{0:T(512)}, u32[]{:S(2)}) copy-start(f32[512]{0:T(512)} %param.14) | copy-start | bytes 6148
  39.5 0.7 %copy-start.5 = (f32[512]{0:T(512)S(1)}, f32[512]{0:T(512)}, u32[]{:S(2)}) copy-start(f32[512]{0:T(512)} %param.15) | copy-start | bytes 6148
  42.9 10.6 %all-to-all-start.2 = ((f32[16,1,128]{2,1,0:T(1,128)}), f32[16,1,128]{2,1,0:T(1,128)S(1)}, u32[]{:S(2)}, u32[]{:S(2)}) async-start(f32[16,1,128]{2,1,0:T(1,128)} %bitcast.8), calls=%async_computation.2 | async-start | bytes 16384 | tf_op jit(solution)/shard_map/all_to_all | solution.py:193
  46.5 7.0 %collective-permute-start.4 = (f32[16,96]{1,0:T(8,128)S(1)}, f32[16,96]{1,0:T(8,128)S(1)}, u32[]{:S(2)}, u32[]{:S(2)}) collective-permute-start(f32[16,96]{1,0:T(8,128)S(1)} %get-tuple-element.14.grad), channel_id=1, source_target_pairs={{0,1},{1,0},{2,3},{3,2},{4,5},{5,4},{6,7},{7,6},{8,9},{9,8},{10,11... | collective-permute-start | bytes 18440 | tf_op jit(solution)/shard_map/ppermute | solution.py:192

commit v2 on v1

v2 whole, which is shorter than its diff:
```python
import math

import jax
import jax.numpy as jnp
from jax import lax
from jax.experimental import pallas as pl
from jax.experimental.pallas import tpu as pltpu
from jax.sharding import PartitionSpec as P

BF16, F32 = jnp.bfloat16, jnp.float32
GROUP = 8
LANES = 128


def mm(a, b):
    return jnp.dot(a, b, preferred_element_type=F32)


class Halves:
    def __init__(self, c, half, w_own, w_oth, layer):
        self.index = (c, 1 - c)
        self.half = half
        self.weights = (w_own, w_oth)
        self.blocks = w_own.shape[0] // 2
        rows = w_own.shape[1] // 2
        self.rows = slice(layer * rows, (layer + 1) * rows)

    def block(self, k, j):
        w = self.weights[j][pl.ds(self.index[k] * self.blocks, self.blocks), self.rows, :]
        return w.reshape(self.half, self.half)

    def cols(self, j):
        return slice(j * self.half, (j + 1) * self.half)

    def vec(self, ref, j):
        return ref[:, pl.ds(pl.multiple_of(self.index[j] * self.half, self.half), self.half)]

    def apply(self, xs, j):
        return mm(xs[0], self.block(0, j)) + mm(xs[1], self.block(1, j))

    def apply_wide(self, xs, j):
        cut = xs[0].shape[0] // 2
        return jnp.concatenate([self.apply([x[:cut] for x in xs], j), self.apply([x[cut:] for x in xs], j)], axis=0)


def natural_order(blocks, out):
    x = lax.axis_index("wx") + len(blocks)
    for d, block in enumerate(blocks):
        out[lax.rem(x - d, len(blocks))] = block[...]


def fetch_kernel(t, v, l, b1, b2, rd, t_mine, vl_own, vecs, sems):
    walkers = v.shape[0]
    rows = t_mine.shape[0]
    mine = lax.axis_index("feat") * rows
    copies = [
        pltpu.make_async_copy(t.at[pl.ds(mine, rows)], t_mine, sems.at[0]),
        pltpu.make_async_copy(v, vl_own.at[pl.ds(0, walkers)], sems.at[1]),
        pltpu.make_async_copy(l, vl_own.at[pl.ds(walkers, walkers)], sems.at[2]),
    ]
    for n, b in enumerate((b1, b2, rd)):
        copies.append(pltpu.make_async_copy(b, vecs.at[n], sems.at[3 + n]))
    for copy in copies:
        copy.start()
    for copy in copies:
        copy.wait()


def block_kernel(got, out):
    peers, layers, rows, _ = got.shape
    for n in range(layers):
        for k in range(peers):
            at = (n * peers + k) * rows
            out[at:at + rows, :] = got[k, n]


def prep_kernel(w1, w2, v, l, sent, pack, w_buf, sems):
    walkers, half = v.shape
    copies = [
        pltpu.make_async_copy(w1, w_buf.at[0], sems.at[0]),
        pltpu.make_async_copy(w2, w_buf.at[1], sems.at[1]),
        pltpu.make_async_copy(v, pack.at[pl.ds(0, walkers)], sems.at[2]),
        pltpu.make_async_copy(l, pack.at[pl.ds(walkers, walkers)], sems.at[3]),
    ]
    for copy in copies:
        copy.start()
    copies[0].wait()
    copies[1].wait()
    for n in (0, 1):
        for k in range(sent.shape[0]):
            h = k % 2
            sent[k, n] = w_buf[n, :, h * half:(h + 1) * half]
    for copy in copies[2:]:
        copy.wait()


def own_columns_kernel(t_own, t_oth, vl_own, vl_oth, w_0, w_1, w_2, w_3, vecs, t2_own, g2_part, aux, w_own):
    walkers = vl_own.shape[0] // 2
    b1, _, _ = (vecs.at[n] for n in range(3))
    mine, per, half = t2_own.shape
    c = lax.axis_index("feat")
    base = c * mine
    natural_order((w_0, w_1, w_2, w_3), w_own)
    one = Halves(c, half, w_own, None, 0)
    two = Halves(c, half, w_own, None, 1)
    aux[:walkers, :] = jnp.tanh(one.apply((vl_own[:walkers, :], vl_oth[:walkers, :]), 0) + one.vec(b1, 0))
    h1 = aux[pl.ds(base, mine), :]
    slope = 1.0 - h1 * h1
    for g in range(mine // GROUP):
        lo, hi = g * GROUP, (g + 1) * GROUP
        ts = (t_own[lo * per:hi * per, :], t_oth[pl.ds((base + lo) * per, GROUP * per), :])
        g1 = one.apply_wide(ts, 0).reshape(GROUP, per, half)
        aux[walkers + lo:walkers + hi, :] = jnp.sum(g1 * g1, axis=1)
        t2 = (g1 * slope[lo:hi, None, :]).astype(BF16)
        t2_own[lo:hi] = t2
        g2_part[lo:hi] = mm(t2.reshape(GROUP * per, half), two.block(0, 0)).reshape(GROUP, per, half)


def rest_kernel(t_own, t_oth, t2_own, g2_part, aux, vl_own, vl_oth, w_own, w_0, w_1, w_2, w_3, vecs,
                amp_out, grad_out, s_out, h_sc, c1_sc, c2_sc, w_oth):
    walkers = vl_own.shape[0] // 2
    b1, b2, rd = (vecs.at[n] for n in range(3))
    mine, per, half = t2_own.shape
    c = lax.axis_index("feat")
    first_z = lax.axis_index("tangent") == 0
    base = c * mine
    natural_order((w_0, w_1, w_2, w_3), w_oth)
    one = Halves(c, half, w_own, w_oth, 0)
    two = Halves(c, half, w_own, w_oth, 1)
    vs = (vl_own[:walkers, :], vl_oth[:walkers, :])
    ls = [vl[pl.ds(walkers + base, mine), :] for vl in (vl_own, vl_oth)]
    vl = [jnp.concatenate([v, l], axis=0) for v, l in zip(vs, ls)]
    pre = one.apply(vl, 1)
    hid = jnp.tanh(pre[:walkers] + one.vec(b1, 1))
    h_sc[:walkers, one.cols(0)] = aux[:walkers, :]
    h_sc[:walkers, one.cols(1)] = hid
    lapin = [one.apply(ls, 0), pre[walkers:]]
    value = [aux[:walkers, :].astype(BF16), hid.astype(BF16)]
    amp = None
    for j in (0, 1):
        hid = jnp.tanh(two.apply(value, j) + two.vec(b2, j))
        h_sc[walkers:, two.cols(j)] = hid
        term = two.vec(rd, j) * hid
        amp = term if amp is None else amp + term
    amp_out[...] = jnp.sum(amp[None], axis=-1)
    h1 = h_sc[pl.ds(base, mine), :]
    h2 = h_sc[pl.ds(walkers + base, mine), :]
    slope1 = 1.0 - h1 * h1
    slope2 = 1.0 - h2 * h2
    rs = [two.vec(rd, j) * slope2[:, two.cols(j)] for j in (0, 1)]
    for g in range(mine // GROUP):
        lo, hi = g * GROUP, (g + 1) * GROUP
        ts = (t_own[lo * per:hi * per, :], t_oth[pl.ds((base + lo) * per, GROUP * per), :])
        g1 = one.apply_wide(ts, 1).reshape(GROUP, per, half)
        c1_sc[lo:hi, :] = jnp.sum(g1 * g1, axis=1)
        t2 = [t2_own[lo:hi].reshape(GROUP * per, half),
              (g1 * slope1[lo:hi, None, one.cols(1)]).astype(BF16).reshape(GROUP * per, half)]
        prod = None
        for j in (0, 1):
            if j == 0:
                g2 = g2_part[lo:hi] + mm(t2[1], two.block(1, 0)).reshape(GROUP, per, half)
            else:
                g2 = two.apply(t2, j).reshape(GROUP, per, half)
            c2_sc[lo:hi, two.cols(j)] = jnp.sum(g2 * g2, axis=1)
            term = g2 * rs[j][lo:hi, None, :]
            prod = term if prod is None else prod + term
        grad_out[lo:hi, :] = jnp.sum(prod, axis=-1)
    curv = [aux[walkers:, :], c1_sc[...]]
    laps = []
    for j in (0, 1):
        s1, h = slope1[:, one.cols(j)], h1[:, one.cols(j)]
        lap = jnp.where(first_z, s1 * lapin[j], 0.0) + (-2.0 * h * s1) * curv[j]
        high = lap.astype(BF16)
        laps.append(jnp.concatenate([high, (lap - high.astype(F32)).astype(BF16)], axis=0))
    total = None
    for j in (0, 1):
        both = two.apply(laps, j)
        h = h2[:, two.cols(j)]
        term = rs[j] * (both[:mine] + both[mine:] + (-2.0 * h) * c2_sc[:, two.cols(j)])
        total = term if total is None else total + term
    gr = grad_out[...]
    row = jnp.sum(total[None], axis=-1) + jnp.sum((gr * gr)[None], axis=-1)
    pair = jnp.concatenate([row, row], axis=1)
    lane = lax.broadcasted_iota(jnp.int32, pair.shape, 1)
    pair = jnp.where((lane >= base) & (lane < base + mine), pair, 0.0)
    s_out[...] = jnp.zeros_like(s_out)
    s_out[:, :walkers] = jnp.broadcast_to(pair, (s_out.shape[0], walkers))


def join_kernel(sums, grad, g_oth, amp, amp_out, grad_out, kin_out):
    mine = grad.shape[0]
    walkers = amp.shape[1]
    c = lax.axis_index("feat")
    amp_out[...] = amp[...]
    grad_out[pl.ds(c * mine, mine), :] = grad[...]
    grad_out[pl.ds((1 - c) * mine, mine), :] = g_oth[...]
    kin_out[...] = -0.5 * sums[:, :walkers]


def in_hbm(x):
    return pltpu.with_memory_space_constraint(x, pltpu.HBM)


def per_device(value_in, tang_in, lap_in, w_first, b_first, w_second, b_second, readout):
    walkers, half = value_in.shape
    per = tang_in.shape[1]
    n_z, n_c = lax.axis_size("tangent"), lax.axis_size("feat")
    n_x, n_y = lax.axis_size("wx"), lax.axis_size("wy")
    mine = walkers // n_c
    peers = n_z * n_c
    rows = w_first.shape[0]
    swap = [(0, 1), (1, 0)]

    flat = tang_in.reshape(walkers * per, half)
    vm = pl.BlockSpec(memory_space=pltpu.VMEM)
    hbm = pl.BlockSpec(memory_space=pltpu.HBM)
    params = pltpu.CompilerParams(vmem_limit_bytes=24 * 1024 * 1024)
    sent, pack = pl.pallas_call(
        prep_kernel,
        out_shape=(
            jax.ShapeDtypeStruct((n_y * peers, 2, rows, half), BF16),
            jax.ShapeDtypeStruct((2 * walkers, half), BF16),
        ),
        in_specs=[hbm] * 4,
        out_specs=(vm, vm),
        scratch_shapes=[pltpu.VMEM((2, rows, n_c * half), BF16), pltpu.SemaphoreType.DMA((4,))],
        compiler_params=params,
        name="prep",
    )(*(in_hbm(x) for x in (w_first, w_second, value_in, lap_in)))
    vl_oth = lax.ppermute(pack, "feat", swap)
    t_oth = lax.ppermute(flat, "feat", swap)
    got = lax.all_to_all(sent, ("wy", "tangent", "feat"), 0, 0, tiled=True)
    block = pl.pallas_call(
        block_kernel,
        out_shape=jax.ShapeDtypeStruct((2 * n_y * peers * rows, half), BF16),
        in_specs=[vm],
        out_specs=vm,
        compiler_params=params,
        name="block",
    )(got)
    near, far = [block] * n_x, [None] * n_x
    for d in (2, 1, 3):
        near[d] = lax.ppermute(block, "wx", [(i, (i + d) % n_x) for i in range(n_x)])
    for d in (0, 2, 1, 3):
        far[d] = lax.ppermute(near[d], "feat", swap)

    width = 2 * half
    t_own, vl_own, vecs = pl.pallas_call(
        fetch_kernel,
        out_shape=(
            jax.ShapeDtypeStruct((mine * per, half), BF16),
            jax.ShapeDtypeStruct((2 * walkers, half), BF16),
            jax.ShapeDtypeStruct((3, 1, width), F32),
        ),
        in_specs=[hbm] * 6,
        out_specs=(vm, vm, vm),
        scratch_shapes=[pltpu.SemaphoreType.DMA((6,))],
        compiler_params=params,
        name="fetch",
    )(*(in_hbm(x) for x in (flat, value_in, lap_in, b_first[None], b_second[None], readout[None])))
    t2_own, g2_part, aux, w_own = pl.pallas_call(
        own_columns_kernel,
        out_shape=(
            jax.ShapeDtypeStruct((mine, per, half), BF16),
            jax.ShapeDtypeStruct((mine, per, half), F32),
            jax.ShapeDtypeStruct((walkers + mine, half), F32),
            jax.ShapeDtypeStruct((n_x,) + block.shape, BF16),
        ),
        in_specs=[vm] * 9,
        out_specs=(vm, vm, vm, vm),
        compiler_params=params,
        cost_estimate=pl.CostEstimate(flops=mine * per * width * width, bytes_accessed=1 << 22, transcendentals=0),
        name="own_columns",
    )(t_own, t_oth, vl_own, vl_oth, *near, vecs)
    amp, grad, part = pl.pallas_call(
        rest_kernel,
        out_shape=(
            jax.ShapeDtypeStruct((1, walkers), F32),
            jax.ShapeDtypeStruct((mine, per), F32),
            jax.ShapeDtypeStruct((peers, LANES), F32),
        ),
        in_specs=[vm] * 13,
        out_specs=(vm, vm, vm),
        scratch_shapes=[
            pltpu.VMEM((2 * walkers, width), F32),
            pltpu.VMEM((mine, half), F32),
            pltpu.VMEM((mine, width), F32),
            pltpu.VMEM((n_x,) + block.shape, BF16),
        ],
        compiler_params=params,
        cost_estimate=pl.CostEstimate(flops=3 * mine * per * width * width, bytes_accessed=1 << 22, transcendentals=0),
        name="rest",
    )(t_own, t_oth, t2_own, g2_part, aux, vl_own, vl_oth, w_own, *far, vecs)

    g_oth = lax.ppermute(grad, "feat", swap)
    sums = lax.all_to_all(part.reshape(peers, 1, LANES), ("tangent", "feat"), 0, 0, tiled=True)
    total = jnp.sum(sums, axis=0)
    amp, gradient, kinetic = pl.pallas_call(
        join_kernel,
        out_shape=(
            jax.ShapeDtypeStruct((1, walkers), F32),
            jax.ShapeDtypeStruct((walkers, per), F32),
            jax.ShapeDtypeStruct((1, walkers), F32),
        ),
        in_specs=[vm] * 4,
        out_specs=(vm, vm, vm),
        compiler_params=pltpu.CompilerParams(vmem_limit_bytes=2 * 1024 * 1024),
        name="join",
    )(total, grad, g_oth, amp)
    return amp.reshape(walkers), gradient, kinetic.reshape(walkers)


def solution(mesh):
    walker, tangent, feat = mesh.devices.shape
    side = math.isqrt(walker)
    mesh = jax.sharding.Mesh(mesh.devices.reshape(side, side, tangent, feat), ("wx", "wy", "tangent", "feat"))
    placed = (
        P(("wx", "wy"), "feat"),
        P(("wx", "wy"), "tangent", "feat"),
        P(("wx", "wy"), "feat"),
        P(("wx", "wy", "tangent", "feat"), None),
        P(),
        P(("wx", "wy", "tangent", "feat"), None),
        P(),
        P(),
    )

    return jax.shard_map(
        per_device,
        mesh=mesh,
        in_specs=placed,
        out_specs=(P(("wx", "wy")), P(("wx", "wy"), "tangent"), P(("wx", "wy"))),
        check_vma=False,
    )
```

time: 54.5 us -> 52.5 us (0.963)
  blocking collectives: 31 us -> 20.2 us
  starting transfers between devices: 9.81 us -> 15.3 us
  Pallas kernels: 3.97 us -> 6.21 us
  waiting for transfers between devices: 7.78 us -> 9.82 us
  other arithmetic: 0.74 us -> 0.03 us
    all_to_all x2 -> x1, blocking collectives: 31 us -> 20.2 us  [per_device(): got = lax.all_to_all(sent, ('wy', 'tangent', 'feat'), 0, 0, tiled=True)]
    ppermute x4 -> x9, starting transfers between devices: 5.87 us -> 11.2 us  [the longest x3 4.89 us: per_device(): lax.ppermute(block, 'wx', [(i, (i + d) % n_x) for i in range(n_x)])]
    pallas_call x0 -> x3, Pallas kernels: none -> 2.11 us  [the longest x1 1.19 us: per_device(): pl.pallas_call(fetch_kernel, out_shape=(jax.ShapeDtypeStruct((mine * per,...]
    ppermute x4 -> x9, waiting for transfers between devices: 1.07 us -> 3.12 us  [the longest x3 2.24 us: per_device(): lax.ppermute(block, 'wx', [(i, (i + d) % n_x) for i in range(n_x)])]
    concatenate x1 -> x0, other arithmetic: 0.71 us -> none  [per_device(): jnp.concatenate([w_first, w_second], axis=0).reshape(2 * rows, n_c, half)]
  transfers between devices with their start and end apart: 6 -> 11, of which waited for: 2 -> 3; matrix products, arithmetic and copies ran while one was open for 2% -> 0% of each run, Pallas kernels for 1% -> 6%
where the time goes in v2:
time: 52.5 us; the launch traced here: 52.2 us
  blocking collectives  20.2 us (38%)
  starting transfers between devices  15.3 us (29%)
  waiting for transfers between devices  9.82 us (19%)
  Pallas kernels  6.21 us (12%)
  between operations  0.7 us (1%)
    all_to_all x1, blocking collectives, per_device(): got = lax.all_to_all(sent, ('wy', 'tangent', 'feat'), 0, 0, tiled=True)  20.2 us
    all_to_all x1, waiting for transfers between devices, per_device(): lax.all_to_all(part.reshape(peers, 1, LANES), ('tangent', 'feat'), 0, 0,...  6.7 us
    ppermute x3, starting transfers between devices, per_device(): lax.ppermute(block, 'wx', [(i, (i + d) % n_x) for i in range(n_x)])  4.89 us
    all_to_all x1, starting transfers between devices, per_device(): lax.all_to_all(part.reshape(peers, 1, LANES), ('tangent', 'feat'), 0, 0,...  3.76 us
    ppermute x1, starting transfers between devices, per_device(): t_oth = lax.ppermute(flat, 'feat', swap)  3.29 us
    pallas_call x1, Pallas kernels, per_device(): pl.pallas_call(rest_kernel, out_shape=(jax.ShapeDtypeStruct((1, walkers),...  2.46 us
    ppermute x3, waiting for transfers between devices, per_device(): lax.ppermute(block, 'wx', [(i, (i + d) % n_x) for i in range(n_x)])  2.24 us
    ppermute x4, starting transfers between devices, per_device(): far[d] = lax.ppermute(near[d], 'feat', swap)  1.77 us
  transfers between devices with their start and end apart: 11, of which 3 were waited for; matrix products, arithmetic and copies ran while one was open for 0% of the time, Pallas kernels for 6%

profile of v2, /device:TPU:1, one launch (start us, length us, event | category | flops | bytes accessed | tf_op | source)
XLA Modules:
  0.0 52.2 jit_solution(8969530891541680729)
XLA Ops:
  0.6 3.3 %collective-permute-start = (bf16[3072,256]{1,0:T(8,128)(2,1)}, bf16[3072,256]{1,0:T(8,128)(2,1)S(1)}, u32[]{:S(2)}, u32[]{:S(2)}) collective-permute-start(bf16[3072,256]{1,0:T(8,128)(2,1)} %bitcast.11), channel_id=1, source_target_pairs={{0,1},{1,0},{2,3},{3,2},{4,5},{5,4},{6,7},{7,6},{8,9},{9,8},{10,11... | collective-permute-start | bytes 4718600 | tf_op jit(solution)/shard_map/ppermute | solution.py:231
  3.9 0.8 %prep.1 = (bf16[64,2,2,256]{3,2,1,0:T(2,128)(2,1)S(1)}, bf16[64,256]{1,0:T(8,128)(2,1)S(1)}) custom-call(bf16[2,512]{1,0:T(2,128)(2,1)} %w1.1, bf16[2,512]{1,0:T(2,128)(2,1)} %w2.1, bf16[32,256]{1,0:T(8,128)(2,1)} %v.3, bf16[32,256]{1,0:T(8,128)(2,1)} %l.3), custom_call_target="tpu_custom_call" | custom-call | tf_op jit(solution)/shard_map/prep/pallas_call | solution.py:218
  4.7 20.2 %all_to_all.10.got = bf16[64,2,2,256]{3,2,1,0:T(2,128)(2,1)S(1)} all-to-all(bf16[64,2,2,256]{3,2,1,0:T(2,128)(2,1)S(1)} %get-tuple-element.21), channel_id=1, replica_groups=mesh['wx'=4,'wy'=4,'tangent'=8,'feat'=2] {'wy','tangent','feat'}, dimensions={0} | all-to-all | bytes 262144 | tf_op jit(solution)/shard_map/all_to_all | solution.py:232
  24.9 0.1 block.1.w_0
  25.0 1.3 %collective-permute-start.2 = (bf16[256,256]{1,0:T(8,128)(2,1)S(1)}, bf16[256,256]{1,0:T(8,128)(2,1)S(1)}, u32[]{:S(2)}, u32[]{:S(2)}) collective-permute-start(bf16[256,256]{1,0:T(8,128)(2,1)S(1)} %block.1.w_0), channel_id=1, source_target_pairs={{0,64},{64,128},{128,192},{192,0},{1,65},{65,129},{129,193},{193,1... | collective-permute-start | bytes 393224 | tf_op jit(solution)/shard_map/ppermute | solution.py:243
  26.3 2.5 %collective-permute-start.3 = (bf16[256,256]{1,0:T(8,128)(2,1)S(1)}, bf16[256,256]{1,0:T(8,128)(2,1)S(1)}, u32[]{:S(2)}, u32[]{:S(2)}) collective-permute-start(bf16[256,256]{1,0:T(8,128)(2,1)S(1)} %block.1.w_0), channel_id=1, source_target_pairs={{0,128},{64,192},{128,0},{192,64},{1,129},{65,193},{129,1},{193,65... | collective-permute-start | bytes 393224 | tf_op jit(solution)/shard_map/ppermute | solution.py:243
  28.8 1.2 %collective-permute-start.4 = (bf16[256,256]{1,0:T(8,128)(2,1)S(1)}, bf16[256,256]{1,0:T(8,128)(2,1)S(1)}, u32[]{:S(2)}, u32[]{:S(2)}) collective-permute-start(bf16[256,256]{1,0:T(8,128)(2,1)S(1)} %block.1.w_0), channel_id=1, source_target_pairs={{0,192},{64,0},{128,64},{192,128},{1,193},{65,1},{129,65},{193,129... | collective-permute-start | bytes 393224 | tf_op jit(solution)/shard_map/ppermute | solution.py:243
  29.9 1.2 %collective-permute-start.1 = (bf16[64,256]{1,0:T(8,128)(2,1)S(1)}, bf16[64,256]{1,0:T(8,128)(2,1)S(1)}, u32[]{:S(2)}, u32[]{:S(2)}) collective-permute-start(bf16[64,256]{1,0:T(8,128)(2,1)S(1)} %get-tuple-element.20), channel_id=1, source_target_pairs={{0,1},{1,0},{2,3},{3,2},{4,5},{5,4},{6,7},{7,6},{8,9},{9,8},{10,11... | collective-permute-start | bytes 98312 | tf_op jit(solution)/shard_map/ppermute | solution.py:230
  31.2 0.9 %collective-permute-done.1.vl_oth = bf16[64,256]{1,0:T(8,128)(2,1)S(1)} collective-permute-done((bf16[64,256]{1,0:T(8,128)(2,1)S(1)}, bf16[64,256]{1,0:T(8,128)(2,1)S(1)}, u32[]{:S(2)}, u32[]{:S(2)}) %collective-permute-start.1) | collective-permute-done | bytes 32800 | tf_op jit(solution)/shard_map/ppermute | solution.py:230
  32.0 0.3 collective-permute-start.5
  32.4 0.0 collective-permute-done.2.w_1
  32.4 0.2 collective-permute-start.6
  32.5 2.2 %collective-permute-done.3.w_2 = bf16[256,256]{1,0:T(8,128)(2,1)S(1)} collective-permute-done((bf16[256,256]{1,0:T(8,128)(2,1)S(1)}, bf16[256,256]{1,0:T(8,128)(2,1)S(1)}, u32[]{:S(2)}, u32[]{:S(2)}) %collective-permute-start.3) | collective-permute-done | bytes 131104 | tf_op jit(solution)/shard_map/ppermute | solution.py:243
  34.8 1.3 %collective-permute-start.7 = (bf16[256,256]{1,0:T(8,128)(2,1)S(1)}, bf16[256,256]{1,0:T(8,128)(2,1)S(1)}, u32[]{:S(2)}, u32[]{:S(2)}) collective-permute-start(bf16[256,256]{1,0:T(8,128)(2,1)S(1)} %collective-permute-done.3.w_2), channel_id=1, source_target_pairs={{0,1},{1,0},{2,3},{3,2},{4,5},{5,4},{6,7},{7,6},{8,9},{9,8},{10,11... | collective-permute-start | bytes 393224 | tf_op jit(solution)/shard_map/ppermute | solution.py:245
  36.0 0.0 collective-permute-done.4.w_3
  36.0 0.0 collective-permute-start.8
  36.0 1.2 %fetch.1 = (bf16[1536,256]{1,0:T(8,128)(2,1)S(1)}, bf16[64,256]{1,0:T(8,128)(2,1)S(1)}, f32[3,1,512]{2,1,0:T(1,128)S(1)}) custom-call(bf16[3072,256]{1,0:T(8,128)(2,1)} %bitcast.12, bf16[32,256]{1,0:T(8,128)(2,1)} %v.3, bf16[32,256]{1,0:T(8,128)(2,1)} %l.3, f32[1,512]{1,0:T(1,128)} %bitcast.13, f32[1,512]{1,0:T(1,128)} %bitcast.14, f32[1,512]{1,0:T(1,128)} %bitcast.15), custom_call_target="tpu_custom_call" | custom-call | tf_op jit(solution)/shard_map/fetch/pallas_call | solution.py:248
  37.2 0.0 collective-permute-done.t_oth
  37.3 1.0 %own_columns.1 = (bf16[16,96,256]{2,1,0:T(8,128)(2,1)S(1)}, f32[16,96,256]{2,1,0:T(8,128)S(1)}, f32[48,256]{1,0:T(8,128)S(1)}, bf16[4,256,256]{2,1,0:T(8,128)(2,1)S(1)}) custom-call(bf16[1536,256]{1,0:T(8,128)(2,1)S(1)} %get-tuple-element.18.t_own, bf16[3072,256]{1,0:T(8,128)(2,1)S(1)} %collective-permute-done.t_oth, ...), custom_call_target="tpu_custom_call" | custom-call | flops 402653184 | bytes 4194304 | tf_op jit(solution)/shard_map/own_columns/pallas_call | solution.py:261
  38.3 0.0 collective-permute-done.5.w_0
  38.3 0.0 collective-permute-done.6.w_1
  38.3 0.0 collective-permute-done.7.w_2
  38.3 0.0 collective-permute-done.8.w_3
  38.3 2.5 %rest.1 = (f32[1,32]{1,0:T(1,128)S(1)}, f32[16,96]{1,0:T(8,128)S(1)}, f32[16,128]{1,0:T(8,128)}) custom-call(bf16[1536,256]{1,0:T(8,128)(2,1)S(1)} %get-tuple-element.18.t_own, bf16[3072,256]{1,0:T(8,128)(2,1)S(1)} %collective-permute-done.t_oth, bf16[16,96,256]{2,1,0:T(8,128)(2,1)S(1)} %get-tuple-element.23.t2_own, ...), custom_call_target="tpu_custom_call" | custom-call | flops 1207959552 | bytes 4194304 | tf_op jit(solution)/shard_map/rest/pallas_call | solution.py:275
  40.8 3.8 %all-to-all-start.1 = ((f32[16,1,128]{2,1,0:T(1,128)}), f32[16,1,128]{2,1,0:T(1,128)S(1)}, u32[]{:S(2)}, u32[]{:S(2)}) async-start(f32[16,1,128]{2,1,0:T(1,128)} %bitcast.5), calls=%async_computation.1 | async-start | bytes 16384 | tf_op jit(solution)/shard_map/all_to_all | solution.py:296
  44.5 0.3 collective-permute-start.9
  44.9 6.7 %all-to-all-done.1 = f32[16,1,128]{2,1,0:T(1,128)S(1)} async-done(((f32[16,1,128]{2,1,0:T(1,128)}), f32[16,1,128]{2,1,0:T(1,128)S(1)}, u32[]{:S(2)}, u32[]{:S(2)}) %all-to-all-start.1) | async-done | bytes 8224 | tf_op jit(solution)/shard_map/all_to_all | solution.py:296
  51.6 0.0 collective-permute-done.9.g_oth
  51.6 0.6 %join.1 = (f32[1,32]{1,0:T(1,128)}, f32[32,96]{1,0:T(8,128)}, f32[1,32]{1,0:T(1,128)}) custom-call(f32[1,128]{1,0:T(1,128)S(1)} %bitcast.10, f32[16,96]{1,0:T(8,128)S(1)} %get-tuple-element.28.grad, f32[16,96]{1,0:T(8,128)S(1)} %collective-permute-done.9.g_oth, f32[1,32]{1,0:T(1,128)S(1)} %get-tuple-element.29.amp), custom_call_target="tpu_custom_call" | custom-call | tf_op jit(solution)/shard_map/join/pallas_call | solution.py:298
  (1 shorter events, 0.0 us)
Async XLA Ops:
  0.6 36.6 %collective-permute-start = (bf16[3072,256]{1,0:T(8,128)(2,1)}, bf16[3072,256]{1,0:T(8,128)(2,1)S(1)}, u32[]{:S(2)}, u32[]{:S(2)}) collective-permute-start(bf16[3072,256]{1,0:T(8,128)(2,1)} %bitcast.11), channel_id=1, source_target_pairs={{0,1},{1,0},{2,3},{3,2},{4,5},{5,4},{6,7},{7,6},{8,9},{9,8},{10,11... | collective-permute-start | bytes 4718600 | tf_op jit(solution)/shard_map/ppermute | solution.py:231
  25.0 7.3 %collective-permute-start.2 = (bf16[256,256]{1,0:T(8,128)(2,1)S(1)}, bf16[256,256]{1,0:T(8,128)(2,1)S(1)}, u32[]{:S(2)}, u32[]{:S(2)}) collective-permute-start(bf16[256,256]{1,0:T(8,128)(2,1)S(1)} %block.1.w_0), channel_id=1, source_target_pairs={{0,64},{64,128},{128,192},{192,0},{1,65},{65,129},{129,193},{193,1... | collective-permute-start | bytes 393224 | tf_op jit(solution)/shard_map/ppermute | solution.py:243
  26.3 8.5 %collective-permute-start.3 = (bf16[256,256]{1,0:T(8,128)(2,1)S(1)}, bf16[256,256]{1,0:T(8,128)(2,1)S(1)}, u32[]{:S(2)}, u32[]{:S(2)}) collective-permute-start(bf16[256,256]{1,0:T(8,128)(2,1)S(1)} %block.1.w_0), channel_id=1, source_target_pairs={{0,128},{64,192},{128,0},{192,64},{1,129},{65,193},{129,1},{193,65... | collective-permute-start | bytes 393224 | tf_op jit(solution)/shard_map/ppermute | solution.py:243
  28.8 7.3 %collective-permute-start.4 = (bf16[256,256]{1,0:T(8,128)(2,1)S(1)}, bf16[256,256]{1,0:T(8,128)(2,1)S(1)}, u32[]{:S(2)}, u32[]{:S(2)}) collective-permute-start(bf16[256,256]{1,0:T(8,128)(2,1)S(1)} %block.1.w_0), channel_id=1, source_target_pairs={{0,192},{64,0},{128,64},{192,128},{1,193},{65,1},{129,65},{193,129... | collective-permute-start | bytes 393224 | tf_op jit(solution)/shard_map/ppermute | solution.py:243
  29.9 2.1 %collective-permute-start.1 = (bf16[64,256]{1,0:T(8,128)(2,1)S(1)}, bf16[64,256]{1,0:T(8,128)(2,1)S(1)}, u32[]{:S(2)}, u32[]{:S(2)}) collective-permute-start(bf16[64,256]{1,0:T(8,128)(2,1)S(1)} %get-tuple-element.20), channel_id=1, source_target_pairs={{0,1},{1,0},{2,3},{3,2},{4,5},{5,4},{6,7},{7,6},{8,9},{9,8},{10,11... | collective-permute-start | bytes 98312 | tf_op jit(solution)/shard_map/ppermute | solution.py:230
  32.0 6.3 %collective-permute-start.5 = (bf16[256,256]{1,0:T(8,128)(2,1)S(1)}, bf16[256,256]{1,0:T(8,128)(2,1)S(1)}, u32[]{:S(2)}, u32[]{:S(2)}) collective-permute-start(bf16[256,256]{1,0:T(8,128)(2,1)S(1)} %block.1.w_0), channel_id=1, source_target_pairs={{0,1},{1,0},{2,3},{3,2},{4,5},{5,4},{6,7},{7,6},{8,9},{9,8},{10,11... | collective-permute-start | bytes 393224 | tf_op jit(solution)/shard_map/ppermute | solution.py:245
  32.4 5.9 %collective-permute-start.6 = (bf16[256,256]{1,0:T(8,128)(2,1)S(1)}, bf16[256,256]{1,0:T(8,128)(2,1)S(1)}, u32[]{:S(2)}, u32[]{:S(2)}) collective-permute-start(bf16[256,256]{1,0:T(8,128)(2,1)S(1)} %collective-permute-done.2.w_1), channel_id=1, source_target_pairs={{0,1},{1,0},{2,3},{3,2},{4,5},{5,4},{6,7},{7,6},{8,9},{9,8},{10,11... | collective-permute-start | bytes 393224 | tf_op jit(solution)/shard_map/ppermute | solution.py:245
  34.8 3.5 %collective-permute-start.7 = (bf16[256,256]{1,0:T(8,128)(2,1)S(1)}, bf16[256,256]{1,0:T(8,128)(2,1)S(1)}, u32[]{:S(2)}, u32[]{:S(2)}) collective-permute-start(bf16[256,256]{1,0:T(8,128)(2,1)S(1)} %collective-permute-done.3.w_2), channel_id=1, source_target_pairs={{0,1},{1,0},{2,3},{3,2},{4,5},{5,4},{6,7},{7,6},{8,9},{9,8},{10,11... | collective-permute-start | bytes 393224 | tf_op jit(solution)/shard_map/ppermute | solution.py:245
  36.0 2.3 %collective-permute-start.8 = (bf16[256,256]{1,0:T(8,128)(2,1)S(1)}, bf16[256,256]{1,0:T(8,128)(2,1)S(1)}, u32[]{:S(2)}, u32[]{:S(2)}) collective-permute-start(bf16[256,256]{1,0:T(8,128)(2,1)S(1)} %collective-permute-done.4.w_3), channel_id=1, source_target_pairs={{0,1},{1,0},{2,3},{3,2},{4,5},{5,4},{6,7},{7,6},{8,9},{9,8},{10,11... | collective-permute-start | bytes 393224 | tf_op jit(solution)/shard_map/ppermute | solution.py:245
  40.8 10.8 %all-to-all-start.1 = ((f32[16,1,128]{2,1,0:T(1,128)}), f32[16,1,128]{2,1,0:T(1,128)S(1)}, u32[]{:S(2)}, u32[]{:S(2)}) async-start(f32[16,1,128]{2,1,0:T(1,128)} %bitcast.5), calls=%async_computation.1 | async-start | bytes 16384 | tf_op jit(solution)/shard_map/all_to_all | solution.py:296
  44.5 7.0 %collective-permute-start.9 = (f32[16,96]{1,0:T(8,128)S(1)}, f32[16,96]{1,0:T(8,128)S(1)}, u32[]{:S(2)}, u32[]{:S(2)}) collective-permute-start(f32[16,96]{1,0:T(8,128)S(1)} %get-tuple-element.28.grad), channel_id=1, source_target_pairs={{0,1},{1,0},{2,3},{3,2},{4,5},{5,4},{6,7},{7,6},{8,9},{9,8},{10,11... | collective-permute-start | bytes 18440 | tf_op jit(solution)/shard_map/ppermute | solution.py:295

commit v3 on v2

--- a/solution.py
+++ b/solution.py
@@ -74,24 +74,16 @@
             out[at:at + rows, :] = got[k, n]
 
 
-def prep_kernel(w1, w2, v, l, sent, pack, w_buf, sems):
-    walkers, half = v.shape
-    copies = [
-        pltpu.make_async_copy(w1, w_buf.at[0], sems.at[0]),
-        pltpu.make_async_copy(w2, w_buf.at[1], sems.at[1]),
-        pltpu.make_async_copy(v, pack.at[pl.ds(0, walkers)], sems.at[2]),
-        pltpu.make_async_copy(l, pack.at[pl.ds(walkers, walkers)], sems.at[3]),
-    ]
+def prep_kernel(w1, w2, sent, w_buf, sems):
+    half = sent.shape[3]
+    copies = [pltpu.make_async_copy(w, w_buf.at[n], sems.at[n]) for n, w in enumerate((w1, w2))]
     for copy in copies:
         copy.start()
-    copies[0].wait()
-    copies[1].wait()
-    for n in (0, 1):
+    for n, copy in enumerate(copies):
+        copy.wait()
         for k in range(sent.shape[0]):
             h = k % 2
             sent[k, n] = w_buf[n, :, h * half:(h + 1) * half]
-    for copy in copies[2:]:
-        copy.wait()
 
 
 def own_columns_kernel(t_own, t_oth, vl_own, vl_oth, w_0, w_1, w_2, w_3, vecs, t2_own, g2_part, aux, w_own):
@@ -215,19 +207,15 @@
     vm = pl.BlockSpec(memory_space=pltpu.VMEM)
     hbm = pl.BlockSpec(memory_space=pltpu.HBM)
     params = pltpu.CompilerParams(vmem_limit_bytes=24 * 1024 * 1024)
-    sent, pack = pl.pallas_call(
+    sent = pl.pallas_call(
         prep_kernel,
-        out_shape=(
-            jax.ShapeDtypeStruct((n_y * peers, 2, rows, half), BF16),
-            jax.ShapeDtypeStruct((2 * walkers, half), BF16),
-        ),
-        in_specs=[hbm] * 4,
-        out_specs=(vm, vm),
-        scratch_shapes=[pltpu.VMEM((2, rows, n_c * half), BF16), pltpu.SemaphoreType.DMA((4,))],
+        out_shape=jax.ShapeDtypeStruct((n_y * peers, 2, rows, half), BF16),
+        in_specs=[hbm] * 2,
+        out_specs=vm,
+        scratch_shapes=[pltpu.VMEM((2, rows, n_c * half), BF16), pltpu.SemaphoreType.DMA((2,))],
         compiler_params=params,
         name="prep",
-    )(*(in_hbm(x) for x in (w_first, w_second, value_in, lap_in)))
-    vl_oth = lax.ppermute(pack, "feat", swap)
+    )(in_hbm(w_first), in_hbm(w_second))
     t_oth = lax.ppermute(flat, "feat", swap)
     got = lax.all_to_all(sent, ("wy", "tangent", "feat"), 0, 0, tiled=True)
     block = pl.pallas_call(
@@ -258,6 +246,7 @@
         compiler_params=params,
         name="fetch",
     )(*(in_hbm(x) for x in (flat, value_in, lap_in, b_first[None], b_second[None], readout[None])))
+    vl_oth = lax.ppermute(vl_own, "feat", swap)
     t2_own, g2_part, aux, w_own = pl.pallas_call(
         own_columns_kernel,
         out_shape=(

time: 52.5 us -> 51.1 us (0.973)
  waiting for transfers between devices: 9.82 us -> 8.82 us
    ppermute x3, waiting for transfers between devices: 2.24 us -> 0.96 us  [per_device(): lax.ppermute(block, 'wx', [(i, (i + d) % n_x) for i in range(n_x)])]
  transfers between devices with their start and end apart: 11 -> 11, of which waited for: 3 -> 4; matrix products, arithmetic and copies ran while one was open for 0% -> 0% of each run, Pallas kernels for 6% -> 6%
where the time goes in v3:
time: 51.1 us; the launch traced here: 50.9 us
  blocking collectives  20.2 us (40%)
  starting transfers between devices  15.1 us (30%)
  waiting for transfers between devices  8.82 us (17%)
  Pallas kernels  6.13 us (12%)
  between operations  0.69 us (1%)
    all_to_all x1, blocking collectives, per_device(): got = lax.all_to_all(sent, ('wy', 'tangent', 'feat'), 0, 0, tiled=True)  20.2 us
    all_to_all x1, waiting for transfers between devices, per_device(): lax.all_to_all(part.reshape(peers, 1, LANES), ('tangent', 'feat'), 0, 0,...  6.7 us
    ppermute x3, starting transfers between devices, per_device(): lax.ppermute(block, 'wx', [(i, (i + d) % n_x) for i in range(n_x)])  4.89 us
    all_to_all x1, starting transfers between devices, per_device(): lax.all_to_all(part.reshape(peers, 1, LANES), ('tangent', 'feat'), 0, 0,...  3.49 us
    ppermute x1, starting transfers between devices, per_device(): t_oth = lax.ppermute(flat, 'feat', swap)  3.29 us
    pallas_call x1, Pallas kernels, per_device(): pl.pallas_call(rest_kernel, out_shape=(jax.ShapeDtypeStruct((1, walkers),...  2.45 us
    ppermute x4, starting transfers between devices, per_device(): far[d] = lax.ppermute(near[d], 'feat', swap)  1.77 us
    ppermute x1, starting transfers between devices, per_device(): vl_oth = lax.ppermute(vl_own, 'feat', swap)  1.32 us
  transfers between devices with their start and end apart: 11, of which 4 were waited for; matrix products, arithmetic and copies ran while one was open for 0% of the time, Pallas kernels for 6%

profile of v3, /device:TPU:1, one launch (start us, length us, event | category | flops | bytes accessed | tf_op | source)
XLA Modules:
  0.0 50.9 jit_solution(15908206404107728051)
XLA Ops:
  0.6 3.3 %collective-permute-start = (bf16[3072,256]{1,0:T(8,128)(2,1)}, bf16[3072,256]{1,0:T(8,128)(2,1)S(1)}, u32[]{:S(2)}, u32[]{:S(2)}) collective-permute-start(bf16[3072,256]{1,0:T(8,128)(2,1)} %bitcast.11), channel_id=1, source_target_pairs={{0,1},{1,0},{2,3},{3,2},{4,5},{5,4},{6,7},{7,6},{8,9},{9,8},{10,11... | collective-permute-start | bytes 4718600 | tf_op jit(solution)/shard_map/ppermute | solution.py:219
  3.9 0.7 %prep.1 = bf16[64,2,2,256]{3,2,1,0:T(2,128)(2,1)S(1)} custom-call(bf16[2,512]{1,0:T(2,128)(2,1)} %w1.1, bf16[2,512]{1,0:T(2,128)(2,1)} %w2.1), custom_call_target="tpu_custom_call" | custom-call | tf_op jit(solution)/shard_map/prep/pallas_call | solution.py:210
  4.7 20.2 %all_to_all.10.got = bf16[64,2,2,256]{3,2,1,0:T(2,128)(2,1)S(1)} all-to-all(bf16[64,2,2,256]{3,2,1,0:T(2,128)(2,1)S(1)} %prep.1), channel_id=1, replica_groups=mesh['wx'=4,'wy'=4,'tangent'=8,'feat'=2] {'wy','tangent','feat'}, dimensions={0} | all-to-all | bytes 262144 | tf_op jit(solution)/shard_map/all_to_all | solution.py:220
  24.9 0.1 block.1.w_0
  25.0 1.3 %collective-permute-start.2 = (bf16[256,256]{1,0:T(8,128)(2,1)S(1)}, bf16[256,256]{1,0:T(8,128)(2,1)S(1)}, u32[]{:S(2)}, u32[]{:S(2)}) collective-permute-start(bf16[256,256]{1,0:T(8,128)(2,1)S(1)} %block.1.w_0), channel_id=1, source_target_pairs={{0,64},{64,128},{128,192},{192,0},{1,65},{65,129},{129,193},{193,1... | collective-permute-start | bytes 393224 | tf_op jit(solution)/shard_map/ppermute | solution.py:231
  26.3 2.5 %collective-permute-start.3 = (bf16[256,256]{1,0:T(8,128)(2,1)S(1)}, bf16[256,256]{1,0:T(8,128)(2,1)S(1)}, u32[]{:S(2)}, u32[]{:S(2)}) collective-permute-start(bf16[256,256]{1,0:T(8,128)(2,1)S(1)} %block.1.w_0), channel_id=1, source_target_pairs={{0,128},{64,192},{128,0},{192,64},{1,129},{65,193},{129,1},{193,65... | collective-permute-start | bytes 393224 | tf_op jit(solution)/shard_map/ppermute | solution.py:231
  28.7 1.2 %collective-permute-start.4 = (bf16[256,256]{1,0:T(8,128)(2,1)S(1)}, bf16[256,256]{1,0:T(8,128)(2,1)S(1)}, u32[]{:S(2)}, u32[]{:S(2)}) collective-permute-start(bf16[256,256]{1,0:T(8,128)(2,1)S(1)} %block.1.w_0), channel_id=1, source_target_pairs={{0,192},{64,0},{128,64},{192,128},{1,193},{65,1},{129,65},{193,129... | collective-permute-start | bytes 393224 | tf_op jit(solution)/shard_map/ppermute | solution.py:231
  29.9 1.2 %fetch.1 = (bf16[1536,256]{1,0:T(8,128)(2,1)S(1)}, bf16[64,256]{1,0:T(8,128)(2,1)S(1)}, f32[3,1,512]{2,1,0:T(1,128)S(1)}) custom-call(bf16[3072,256]{1,0:T(8,128)(2,1)} %bitcast.12, bf16[32,256]{1,0:T(8,128)(2,1)} %v.1, bf16[32,256]{1,0:T(8,128)(2,1)} %l.1, f32[1,512]{1,0:T(1,128)} %bitcast.13, f32[1,512]{1,0:T(1,128)} %bitcast.14, f32[1,512]{1,0:T(1,128)} %bitcast.15), custom_call_target="tpu_custom_call" | custom-call | tf_op jit(solution)/shard_map/fetch/pallas_call | solution.py:236
  31.1 1.3 %collective-permute-start.1 = (bf16[64,256]{1,0:T(8,128)(2,1)S(1)}, bf16[64,256]{1,0:T(8,128)(2,1)S(1)}, u32[]{:S(2)}, u32[]{:S(2)}) collective-permute-start(bf16[64,256]{1,0:T(8,128)(2,1)S(1)} %get-tuple-element.17.vl_own), channel_id=1, source_target_pairs={{0,1},{1,0},{2,3},{3,2},{4,5},{5,4},{6,7},{7,6},{8,9},{9,8},{10,11... | collective-permute-start | bytes 98312 | tf_op jit(solution)/shard_map/ppermute | solution.py:249
  32.4 0.9 %collective-permute-done.1.vl_oth = bf16[64,256]{1,0:T(8,128)(2,1)S(1)} collective-permute-done((bf16[64,256]{1,0:T(8,128)(2,1)S(1)}, bf16[64,256]{1,0:T(8,128)(2,1)S(1)}, u32[]{:S(2)}, u32[]{:S(2)}) %collective-permute-start.1) | collective-permute-done | bytes 32800 | tf_op jit(solution)/shard_map/ppermute | solution.py:249
  33.3 0.3 collective-permute-start.5
  33.6 0.0 collective-permute-done.2.w_1
  33.6 0.2 collective-permute-start.6
  33.8 1.0 %collective-permute-done.3.w_2 = bf16[256,256]{1,0:T(8,128)(2,1)S(1)} collective-permute-done((bf16[256,256]{1,0:T(8,128)(2,1)S(1)}, bf16[256,256]{1,0:T(8,128)(2,1)S(1)}, u32[]{:S(2)}, u32[]{:S(2)}) %collective-permute-start.3) | collective-permute-done | bytes 131104 | tf_op jit(solution)/shard_map/ppermute | solution.py:231
  34.7 1.3 %collective-permute-start.7 = (bf16[256,256]{1,0:T(8,128)(2,1)S(1)}, bf16[256,256]{1,0:T(8,128)(2,1)S(1)}, u32[]{:S(2)}, u32[]{:S(2)}) collective-permute-start(bf16[256,256]{1,0:T(8,128)(2,1)S(1)} %collective-permute-done.3.w_2), channel_id=1, source_target_pairs={{0,1},{1,0},{2,3},{3,2},{4,5},{5,4},{6,7},{7,6},{8,9},{9,8},{10,11... | collective-permute-start | bytes 393224 | tf_op jit(solution)/shard_map/ppermute | solution.py:233
  36.0 0.0 collective-permute-done.4.w_3
  36.0 0.0 collective-permute-start.8
  36.0 0.0 collective-permute-done.t_oth
  36.0 1.0 %own_columns.1 = (bf16[16,96,256]{2,1,0:T(8,128)(2,1)S(1)}, f32[16,96,256]{2,1,0:T(8,128)S(1)}, f32[48,256]{1,0:T(8,128)S(1)}, bf16[4,256,256]{2,1,0:T(8,128)(2,1)S(1)}) custom-call(bf16[1536,256]{1,0:T(8,128)(2,1)S(1)} %get-tuple-element.16.t_own, bf16[3072,256]{1,0:T(8,128)(2,1)S(1)} %collective-permute-done.t_oth, ...), custom_call_target="tpu_custom_call" | custom-call | flops 402653184 | bytes 4194304 | tf_op jit(solution)/shard_map/own_columns/pallas_call | solution.py:250
  37.0 0.0 collective-permute-done.5.w_0
  37.0 0.0 collective-permute-done.6.w_1
  37.0 0.0 collective-permute-done.7.w_2
  37.0 0.3 collective-permute-done.8.w_3
  37.3 2.5 %rest.1 = (f32[1,32]{1,0:T(1,128)S(1)}, f32[16,96]{1,0:T(8,128)S(1)}, f32[16,128]{1,0:T(8,128)}) custom-call(bf16[1536,256]{1,0:T(8,128)(2,1)S(1)} %get-tuple-element.16.t_own, bf16[3072,256]{1,0:T(8,128)(2,1)S(1)} %collective-permute-done.t_oth, bf16[16,96,256]{2,1,0:T(8,128)(2,1)S(1)} %get-tuple-element.19.t2_own, ...), custom_call_target="tpu_custom_call" | custom-call | flops 1207959552 | bytes 4194304 | tf_op jit(solution)/shard_map/rest/pallas_call | solution.py:264
  39.8 3.5 %all-to-all-start.1 = ((f32[16,1,128]{2,1,0:T(1,128)}), f32[16,1,128]{2,1,0:T(1,128)S(1)}, u32[]{:S(2)}, u32[]{:S(2)}) async-start(f32[16,1,128]{2,1,0:T(1,128)} %bitcast.5), calls=%async_computation.1 | async-start | bytes 16384 | tf_op jit(solution)/shard_map/all_to_all | solution.py:285
  43.3 0.3 collective-permute-start.9
  43.6 6.7 %all-to-all-done.1 = f32[16,1,128]{2,1,0:T(1,128)S(1)} async-done(((f32[16,1,128]{2,1,0:T(1,128)}), f32[16,1,128]{2,1,0:T(1,128)S(1)}, u32[]{:S(2)}, u32[]{:S(2)}) %all-to-all-start.1) | async-done | bytes 8224 | tf_op jit(solution)/shard_map/all_to_all | solution.py:285
  50.3 0.0 collective-permute-done.9.g_oth
  50.3 0.6 %join.1 = (f32[1,32]{1,0:T(1,128)}, f32[32,96]{1,0:T(8,128)}, f32[1,32]{1,0:T(1,128)}) custom-call(f32[1,128]{1,0:T(1,128)S(1)} %bitcast.10, f32[16,96]{1,0:T(8,128)S(1)} %get-tuple-element.24.grad, f32[16,96]{1,0:T(8,128)S(1)} %collective-permute-done.9.g_oth, f32[1,32]{1,0:T(1,128)S(1)} %get-tuple-element.25.amp), custom_call_target="tpu_custom_call" | custom-call | tf_op jit(solution)/shard_map/join/pallas_call | solution.py:287
  (1 shorter events, 0.0 us)
Async XLA Ops:
  0.6 35.4 %collective-permute-start = (bf16[3072,256]{1,0:T(8,128)(2,1)}, bf16[3072,256]{1,0:T(8,128)(2,1)S(1)}, u32[]{:S(2)}, u32[]{:S(2)}) collective-permute-start(bf16[3072,256]{1,0:T(8,128)(2,1)} %bitcast.11), channel_id=1, source_target_pairs={{0,1},{1,0},{2,3},{3,2},{4,5},{5,4},{6,7},{7,6},{8,9},{9,8},{10,11... | collective-permute-start | bytes 4718600 | tf_op jit(solution)/shard_map/ppermute | solution.py:219
  25.0 8.6 %collective-permute-start.2 = (bf16[256,256]{1,0:T(8,128)(2,1)S(1)}, bf16[256,256]{1,0:T(8,128)(2,1)S(1)}, u32[]{:S(2)}, u32[]{:S(2)}) collective-permute-start(bf16[256,256]{1,0:T(8,128)(2,1)S(1)} %block.1.w_0), channel_id=1, source_target_pairs={{0,64},{64,128},{128,192},{192,0},{1,65},{65,129},{129,193},{193,1... | collective-permute-start | bytes 393224 | tf_op jit(solution)/shard_map/ppermute | solution.py:231
  26.3 8.5 %collective-permute-start.3 = (bf16[256,256]{1,0:T(8,128)(2,1)S(1)}, bf16[256,256]{1,0:T(8,128)(2,1)S(1)}, u32[]{:S(2)}, u32[]{:S(2)}) collective-permute-start(bf16[256,256]{1,0:T(8,128)(2,1)S(1)} %block.1.w_0), channel_id=1, source_target_pairs={{0,128},{64,192},{128,0},{192,64},{1,129},{65,193},{129,1},{193,65... | collective-permute-start | bytes 393224 | tf_op jit(solution)/shard_map/ppermute | solution.py:231
  28.7 7.3 %collective-permute-start.4 = (bf16[256,256]{1,0:T(8,128)(2,1)S(1)}, bf16[256,256]{1,0:T(8,128)(2,1)S(1)}, u32[]{:S(2)}, u32[]{:S(2)}) collective-permute-start(bf16[256,256]{1,0:T(8,128)(2,1)S(1)} %block.1.w_0), channel_id=1, source_target_pairs={{0,192},{64,0},{128,64},{192,128},{1,193},{65,1},{129,65},{193,129... | collective-permute-start | bytes 393224 | tf_op jit(solution)/shard_map/ppermute | solution.py:231
  31.1 2.2 %collective-permute-start.1 = (bf16[64,256]{1,0:T(8,128)(2,1)S(1)}, bf16[64,256]{1,0:T(8,128)(2,1)S(1)}, u32[]{:S(2)}, u32[]{:S(2)}) collective-permute-start(bf16[64,256]{1,0:T(8,128)(2,1)S(1)} %get-tuple-element.17.vl_own), channel_id=1, source_target_pairs={{0,1},{1,0},{2,3},{3,2},{4,5},{5,4},{6,7},{7,6},{8,9},{9,8},{10,11... | collective-permute-start | bytes 98312 | tf_op jit(solution)/shard_map/ppermute | solution.py:249
  33.3 3.8 %collective-permute-start.5 = (bf16[256,256]{1,0:T(8,128)(2,1)S(1)}, bf16[256,256]{1,0:T(8,128)(2,1)S(1)}, u32[]{:S(2)}, u32[]{:S(2)}) collective-permute-start(bf16[256,256]{1,0:T(8,128)(2,1)S(1)} %block.1.w_0), channel_id=1, source_target_pairs={{0,1},{1,0},{2,3},{3,2},{4,5},{5,4},{6,7},{7,6},{8,9},{9,8},{10,11... | collective-permute-start | bytes 393224 | tf_op jit(solution)/shard_map/ppermute | solution.py:233
  33.6 3.4 %collective-permute-start.6 = (bf16[256,256]{1,0:T(8,128)(2,1)S(1)}, bf16[256,256]{1,0:T(8,128)(2,1)S(1)}, u32[]{:S(2)}, u32[]{:S(2)}) collective-permute-start(bf16[256,256]{1,0:T(8,128)(2,1)S(1)} %collective-permute-done.2.w_1), channel_id=1, source_target_pairs={{0,1},{1,0},{2,3},{3,2},{4,5},{5,4},{6,7},{7,6},{8,9},{9,8},{10,11... | collective-permute-start | bytes 393224 | tf_op jit(solution)/shard_map/ppermute | solution.py:233
  34.7 2.3 %collective-permute-start.7 = (bf16[256,256]{1,0:T(8,128)(2,1)S(1)}, bf16[256,256]{1,0:T(8,128)(2,1)S(1)}, u32[]{:S(2)}, u32[]{:S(2)}) collective-permute-start(bf16[256,256]{1,0:T(8,128)(2,1)S(1)} %collective-permute-done.3.w_2), channel_id=1, source_target_pairs={{0,1},{1,0},{2,3},{3,2},{4,5},{5,4},{6,7},{7,6},{8,9},{9,8},{10,11... | collective-permute-start | bytes 393224 | tf_op jit(solution)/shard_map/ppermute | solution.py:233
  36.0 1.3 %collective-permute-start.8 = (bf16[256,256]{1,0:T(8,128)(2,1)S(1)}, bf16[256,256]{1,0:T(8,128)(2,1)S(1)}, u32[]{:S(2)}, u32[]{:S(2)}) collective-permute-start(bf16[256,256]{1,0:T(8,128)(2,1)S(1)} %collective-permute-done.4.w_3), channel_id=1, source_target_pairs={{0,1},{1,0},{2,3},{3,2},{4,5},{5,4},{6,7},{7,6},{8,9},{9,8},{10,11... | collective-permute-start | bytes 393224 | tf_op jit(solution)/shard_map/ppermute | solution.py:233
  39.8 10.5 %all-to-all-start.1 = ((f32[16,1,128]{2,1,0:T(1,128)}), f32[16,1,128]{2,1,0:T(1,128)S(1)}, u32[]{:S(2)}, u32[]{:S(2)}) async-start(f32[16,1,128]{2,1,0:T(1,128)} %bitcast.5), calls=%async_computation.1 | async-start | bytes 16384 | tf_op jit(solution)/shard_map/all_to_all | solution.py:285
  43.3 7.0 %collective-permute-start.9 = (f32[16,96]{1,0:T(8,128)S(1)}, f32[16,96]{1,0:T(8,128)S(1)}, u32[]{:S(2)}, u32[]{:S(2)}) collective-permute-start(f32[16,96]{1,0:T(8,128)S(1)} %get-tuple-element.24.grad), channel_id=1, source_target_pairs={{0,1},{1,0},{2,3},{3,2},{4,5},{5,4},{6,7},{7,6},{8,9},{9,8},{10,11... | collective-permute-start | bytes 18440 | tf_op jit(solution)/shard_map/ppermute | solution.py:284

commit v4 on v3

--- a/solution.py
+++ b/solution.py
@@ -16,17 +16,21 @@
     return jnp.dot(a, b, preferred_element_type=F32)
 
 
+def mm_wide(a, b):
+    cut = a.shape[0] // 2
+    return jnp.concatenate([mm(a[:cut], b), mm(a[cut:], b)], axis=0)
+
+
 class Halves:
     def __init__(self, c, half, w_own, w_oth, layer):
         self.index = (c, 1 - c)
         self.half = half
         self.weights = (w_own, w_oth)
         self.blocks = w_own.shape[0] // 2
-        rows = w_own.shape[1] // 2
-        self.rows = slice(layer * rows, (layer + 1) * rows)
+        self.layer = layer
 
     def block(self, k, j):
-        w = self.weights[j][pl.ds(self.index[k] * self.blocks, self.blocks), self.rows, :]
+        w = self.weights[j][pl.ds(self.index[k] * self.blocks, self.blocks), self.layer]
         return w.reshape(self.half, self.half)
 
     def cols(self, j):
@@ -44,9 +48,13 @@
 
 
 def natural_order(blocks, out):
-    x = lax.axis_index("wx") + len(blocks)
+    y = lax.axis_index("wy") + len(blocks)
+    n_x, layers, _, rows, _ = out.shape
     for d, block in enumerate(blocks):
-        out[lax.rem(x - d, len(blocks))] = block[...]
+        for n in range(layers):
+            for k in range(n_x):
+                at = (n * n_x + k) * rows
+                out[k, n, lax.rem(y - d, len(blocks))] = block[at:at + rows, :]
 
 
 def fetch_kernel(t, v, l, b1, b2, rd, t_mine, vl_own, vecs, sems):
@@ -105,7 +113,7 @@
         aux[walkers + lo:walkers + hi, :] = jnp.sum(g1 * g1, axis=1)
         t2 = (g1 * slope[lo:hi, None, :]).astype(BF16)
         t2_own[lo:hi] = t2
-        g2_part[lo:hi] = mm(t2.reshape(GROUP * per, half), two.block(0, 0)).reshape(GROUP, per, half)
+        g2_part[lo:hi] = mm_wide(t2.reshape(GROUP * per, half), two.block(0, 0)).reshape(GROUP, per, half)
 
 
 def rest_kernel(t_own, t_oth, t2_own, g2_part, aux, vl_own, vl_oth, w_own, w_0, w_1, w_2, w_3, vecs,
@@ -119,14 +127,42 @@
     natural_order((w_0, w_1, w_2, w_3), w_oth)
     one = Halves(c, half, w_own, w_oth, 0)
     two = Halves(c, half, w_own, w_oth, 1)
+    left, right = one.cols(0), one.cols(1)
+
+    def layer_one(g):
+        lo, hi = g * GROUP, (g + 1) * GROUP
+        ts = (t_own[lo * per:hi * per, :], t_oth[pl.ds((base + lo) * per, GROUP * per), :])
+        return one.apply_wide(ts, 1).reshape(GROUP, per, half)
+
+    def finish_one(g, g1):
+        lo, hi = g * GROUP, (g + 1) * GROUP
+        c1_sc[lo:hi, :] = jnp.sum(g1 * g1, axis=1)
+        return (g1 * slope1[lo:hi, None, right]).astype(BF16).reshape(GROUP * per, half)
+
+    def layer_two(g, far):
+        lo, hi = g * GROUP, (g + 1) * GROUP
+        near = t2_own[lo:hi].reshape(GROUP * per, half)
+        prod = None
+        for j in (0, 1):
+            if j == 0:
+                g2 = g2_part[lo:hi] + mm_wide(far, two.block(1, 0)).reshape(GROUP, per, half)
+            else:
+                g2 = two.apply_wide((near, far), 1).reshape(GROUP, per, half)
+            c2_sc[lo:hi, two.cols(j)] = jnp.sum(g2 * g2, axis=1)
+            term = g2 * rs[j][lo:hi, None, :]
+            prod = term if prod is None else prod + term
+        grad_out[lo:hi, :] = jnp.sum(prod, axis=-1)
+
     vs = (vl_own[:walkers, :], vl_oth[:walkers, :])
     ls = [vl[pl.ds(walkers + base, mine), :] for vl in (vl_own, vl_oth)]
-    vl = [jnp.concatenate([v, l], axis=0) for v, l in zip(vs, ls)]
-    pre = one.apply(vl, 1)
+    pre = one.apply([jnp.concatenate([v, l], axis=0) for v, l in zip(vs, ls)], 1)
+    lapin = [one.apply(ls, 0), pre[walkers:]]
+    g1 = layer_one(0)
     hid = jnp.tanh(pre[:walkers] + one.vec(b1, 1))
-    h_sc[:walkers, one.cols(0)] = aux[:walkers, :]
-    h_sc[:walkers, one.cols(1)] = hid
-    lapin = [one.apply(ls, 0), pre[walkers:]]
+    h_sc[:walkers, left] = aux[:walkers, :]
+    h_sc[:walkers, right] = hid
+    h1 = h_sc[pl.ds(base, mine), :]
+    slope1 = 1.0 - h1 * h1
     value = [aux[:walkers, :].astype(BF16), hid.astype(BF16)]
     amp = None
     for j in (0, 1):
@@ -135,28 +171,12 @@
         term = two.vec(rd, j) * hid
         amp = term if amp is None else amp + term
     amp_out[...] = jnp.sum(amp[None], axis=-1)
-    h1 = h_sc[pl.ds(base, mine), :]
     h2 = h_sc[pl.ds(walkers + base, mine), :]
-    slope1 = 1.0 - h1 * h1
     slope2 = 1.0 - h2 * h2
     rs = [two.vec(rd, j) * slope2[:, two.cols(j)] for j in (0, 1)]
     for g in range(mine // GROUP):
-        lo, hi = g * GROUP, (g + 1) * GROUP
-        ts = (t_own[lo * per:hi * per, :], t_oth[pl.ds((base + lo) * per, GROUP * per), :])
-        g1 = one.apply_wide(ts, 1).reshape(GROUP, per, half)
-        c1_sc[lo:hi, :] = jnp.sum(g1 * g1, axis=1)
-        t2 = [t2_own[lo:hi].reshape(GROUP * per, half),
-              (g1 * slope1[lo:hi, None, one.cols(1)]).astype(BF16).reshape(GROUP * per, half)]
-        prod = None
-        for j in (0, 1):
-            if j == 0:
-                g2 = g2_part[lo:hi] + mm(t2[1], two.block(1, 0)).reshape(GROUP, per, half)
-            else:
-                g2 = two.apply(t2, j).reshape(GROUP, per, half)
-            c2_sc[lo:hi, two.cols(j)] = jnp.sum(g2 * g2, axis=1)
-            term = g2 * rs[j][lo:hi, None, :]
-            prod = term if prod is None else prod + term
-        grad_out[lo:hi, :] = jnp.sum(prod, axis=-1)
+        far = finish_one(g, g1 if g == 0 else layer_one(g))
+        layer_two(g, far)
     curv = [aux[walkers:, :], c1_sc[...]]
     laps = []
     for j in (0, 1):
@@ -164,11 +184,11 @@
         lap = jnp.where(first_z, s1 * lapin[j], 0.0) + (-2.0 * h * s1) * curv[j]
         high = lap.astype(BF16)
         laps.append(jnp.concatenate([high, (lap - high.astype(F32)).astype(BF16)], axis=0))
+    lapin2 = [two.apply(laps, j) for j in (0, 1)]
     total = None
     for j in (0, 1):
-        both = two.apply(laps, j)
         h = h2[:, two.cols(j)]
-        term = rs[j] * (both[:mine] + both[mine:] + (-2.0 * h) * c2_sc[:, two.cols(j)])
+        term = rs[j] * (lapin2[j][:mine] + lapin2[j][mine:] + (-2.0 * h) * c2_sc[:, two.cols(j)])
         total = term if total is None else total + term
     gr = grad_out[...]
     row = jnp.sum(total[None], axis=-1) + jnp.sum((gr * gr)[None], axis=-1)
@@ -209,7 +229,7 @@
     params = pltpu.CompilerParams(vmem_limit_bytes=24 * 1024 * 1024)
     sent = pl.pallas_call(
         prep_kernel,
-        out_shape=jax.ShapeDtypeStruct((n_y * peers, 2, rows, half), BF16),
+        out_shape=jax.ShapeDtypeStruct((n_x * peers, 2, rows, half), BF16),
         in_specs=[hbm] * 2,
         out_specs=vm,
         scratch_shapes=[pltpu.VMEM((2, rows, n_c * half), BF16), pltpu.SemaphoreType.DMA((2,))],
@@ -217,18 +237,18 @@
         name="prep",
     )(in_hbm(w_first), in_hbm(w_second))
     t_oth = lax.ppermute(flat, "feat", swap)
-    got = lax.all_to_all(sent, ("wy", "tangent", "feat"), 0, 0, tiled=True)
+    got = lax.all_to_all(sent, ("wx", "tangent", "feat"), 0, 0, tiled=True)
     block = pl.pallas_call(
         block_kernel,
-        out_shape=jax.ShapeDtypeStruct((2 * n_y * peers * rows, half), BF16),
+        out_shape=jax.ShapeDtypeStruct((2 * n_x * peers * rows, half), BF16),
         in_specs=[vm],
         out_specs=vm,
         compiler_params=params,
         name="block",
     )(got)
-    near, far = [block] * n_x, [None] * n_x
+    near, far = [block] * n_y, [None] * n_y
     for d in (2, 1, 3):
-        near[d] = lax.ppermute(block, "wx", [(i, (i + d) % n_x) for i in range(n_x)])
+        near[d] = lax.ppermute(block, "wy", [(i, (i + d) % n_y) for i in range(n_y)])
     for d in (0, 2, 1, 3):
         far[d] = lax.ppermute(near[d], "feat", swap)
 
@@ -253,7 +273,7 @@
             jax.ShapeDtypeStruct((mine, per, half), BF16),
             jax.ShapeDtypeStruct((mine, per, half), F32),
             jax.ShapeDtypeStruct((walkers + mine, half), F32),
-            jax.ShapeDtypeStruct((n_x,) + block.shape, BF16),
+            jax.ShapeDtypeStruct((n_x, 2, n_y, peers * rows, half), BF16),
         ),
         in_specs=[vm] * 9,
         out_specs=(vm, vm, vm, vm),
@@ -274,7 +294,7 @@
             pltpu.VMEM((2 * walkers, width), F32),
             pltpu.VMEM((mine, half), F32),
             pltpu.VMEM((mine, width), F32),
-            pltpu.VMEM((n_x,) + block.shape, BF16),
+            pltpu.VMEM((n_x, 2, n_y, peers * rows, half), BF16),
         ],
         compiler_params=params,
         cost_estimate=pl.CostEstimate(flops=3 * mine * per * width * width, bytes_accessed=1 << 22, transcendentals=0),

time: 51.1 us -> 51 us (level)
  no operation moved by 1% of the time
where the time goes in v4:
time: 51 us; the launch traced here: 50.8 us
  blocking collectives  20 us (39%)
  starting transfers between devices  15.2 us (30%)
  waiting for transfers between devices  8.94 us (18%)
  Pallas kernels  5.96 us (12%)
  between operations  0.69 us (1%)
    all_to_all x1, blocking collectives, per_device(): got = lax.all_to_all(sent, ('wx', 'tangent', 'feat'), 0, 0, tiled=True)  20 us
    all_to_all x1, waiting for transfers between devices, per_device(): lax.all_to_all(part.reshape(peers, 1, LANES), ('tangent', 'feat'), 0, 0,...  6.7 us
    ppermute x3, starting transfers between devices, per_device(): lax.ppermute(block, 'wy', [(i, (i + d) % n_y) for i in range(n_y)])  5.06 us
    all_to_all x1, starting transfers between devices, per_device(): lax.all_to_all(part.reshape(peers, 1, LANES), ('tangent', 'feat'), 0, 0,...  3.45 us
    ppermute x1, starting transfers between devices, per_device(): t_oth = lax.ppermute(flat, 'feat', swap)  3.29 us
    pallas_call x1, Pallas kernels, per_device(): pl.pallas_call(rest_kernel, out_shape=(jax.ShapeDtypeStruct((1, walkers),...  2.32 us
    ppermute x4, starting transfers between devices, per_device(): far[d] = lax.ppermute(near[d], 'feat', swap)  1.77 us
    ppermute x1, starting transfers between devices, per_device(): vl_oth = lax.ppermute(vl_own, 'feat', swap)  1.32 us
  transfers between devices with their start and end apart: 11, of which 4 were waited for; matrix products, arithmetic and copies ran while one was open for 0% of the time, Pallas kernels for 6%

profile of v4, /device:TPU:1, one launch (start us, length us, event | category | flops | bytes accessed | tf_op | source)
XLA Modules:
  0.0 50.8 jit_solution(9617034272935083958)
XLA Ops:
  0.6 3.3 %collective-permute-start = (bf16[3072,256]{1,0:T(8,128)(2,1)}, bf16[3072,256]{1,0:T(8,128)(2,1)S(1)}, u32[]{:S(2)}, u32[]{:S(2)}) collective-permute-start(bf16[3072,256]{1,0:T(8,128)(2,1)} %bitcast.11), channel_id=1, source_target_pairs={{0,1},{1,0},{2,3},{3,2},{4,5},{5,4},{6,7},{7,6},{8,9},{9,8},{10,11... | collective-permute-start | bytes 4718600 | tf_op jit(solution)/shard_map/ppermute | solution.py:239
  3.9 0.7 %prep.1 = bf16[64,2,2,256]{3,2,1,0:T(2,128)(2,1)S(1)} custom-call(bf16[2,512]{1,0:T(2,128)(2,1)} %w1.1, bf16[2,512]{1,0:T(2,128)(2,1)} %w2.1), custom_call_target="tpu_custom_call" | custom-call | tf_op jit(solution)/shard_map/prep/pallas_call | solution.py:230
  4.7 20.0 %all_to_all.10.got = bf16[64,2,2,256]{3,2,1,0:T(2,128)(2,1)S(1)} all-to-all(bf16[64,2,2,256]{3,2,1,0:T(2,128)(2,1)S(1)} %prep.1), channel_id=1, replica_groups=mesh['wx'=4,'wy'=4,'tangent'=8,'feat'=2] {'wx','tangent','feat'}, dimensions={0} | all-to-all | bytes 262144 | tf_op jit(solution)/shard_map/all_to_all | solution.py:240
  24.7 0.1 block.1.w_0
  24.8 1.4 %collective-permute-start.2 = (bf16[256,256]{1,0:T(8,128)(2,1)S(1)}, bf16[256,256]{1,0:T(8,128)(2,1)S(1)}, u32[]{:S(2)}, u32[]{:S(2)}) collective-permute-start(bf16[256,256]{1,0:T(8,128)(2,1)S(1)} %block.1.w_0), channel_id=1, source_target_pairs={{0,16},{16,32},{32,48},{48,0},{1,17},{17,33},{33,49},{49,1},{2,18}... | collective-permute-start | bytes 393224 | tf_op jit(solution)/shard_map/ppermute | solution.py:251
  26.2 2.6 %collective-permute-start.3 = (bf16[256,256]{1,0:T(8,128)(2,1)S(1)}, bf16[256,256]{1,0:T(8,128)(2,1)S(1)}, u32[]{:S(2)}, u32[]{:S(2)}) collective-permute-start(bf16[256,256]{1,0:T(8,128)(2,1)S(1)} %block.1.w_0), channel_id=1, source_target_pairs={{0,32},{16,48},{32,0},{48,16},{1,33},{17,49},{33,1},{49,17},{2,34}... | collective-permute-start | bytes 393224 | tf_op jit(solution)/shard_map/ppermute | solution.py:251
  28.8 1.1 %collective-permute-start.4 = (bf16[256,256]{1,0:T(8,128)(2,1)S(1)}, bf16[256,256]{1,0:T(8,128)(2,1)S(1)}, u32[]{:S(2)}, u32[]{:S(2)}) collective-permute-start(bf16[256,256]{1,0:T(8,128)(2,1)S(1)} %block.1.w_0), channel_id=1, source_target_pairs={{0,48},{16,0},{32,16},{48,32},{1,49},{17,1},{33,17},{49,33},{2,50}... | collective-permute-start | bytes 393224 | tf_op jit(solution)/shard_map/ppermute | solution.py:251
  29.9 1.2 %fetch.1 = (bf16[1536,256]{1,0:T(8,128)(2,1)S(1)}, bf16[64,256]{1,0:T(8,128)(2,1)S(1)}, f32[3,1,512]{2,1,0:T(1,128)S(1)}) custom-call(bf16[3072,256]{1,0:T(8,128)(2,1)} %bitcast.12, bf16[32,256]{1,0:T(8,128)(2,1)} %v.1, bf16[32,256]{1,0:T(8,128)(2,1)} %l.1, f32[1,512]{1,0:T(1,128)} %bitcast.13, f32[1,512]{1,0:T(1,128)} %bitcast.14, f32[1,512]{1,0:T(1,128)} %bitcast.15), custom_call_target="tpu_custom_call" | custom-call | tf_op jit(solution)/shard_map/fetch/pallas_call | solution.py:256
  31.1 1.3 %collective-permute-start.1 = (bf16[64,256]{1,0:T(8,128)(2,1)S(1)}, bf16[64,256]{1,0:T(8,128)(2,1)S(1)}, u32[]{:S(2)}, u32[]{:S(2)}) collective-permute-start(bf16[64,256]{1,0:T(8,128)(2,1)S(1)} %get-tuple-element.17.vl_own), channel_id=1, source_target_pairs={{0,1},{1,0},{2,3},{3,2},{4,5},{5,4},{6,7},{7,6},{8,9},{9,8},{10,11... | collective-permute-start | bytes 98312 | tf_op jit(solution)/shard_map/ppermute | solution.py:269
  32.4 0.9 %collective-permute-done.1.vl_oth = bf16[64,256]{1,0:T(8,128)(2,1)S(1)} collective-permute-done((bf16[64,256]{1,0:T(8,128)(2,1)S(1)}, bf16[64,256]{1,0:T(8,128)(2,1)S(1)}, u32[]{:S(2)}, u32[]{:S(2)}) %collective-permute-start.1) | collective-permute-done | bytes 32800 | tf_op jit(solution)/shard_map/ppermute | solution.py:269
  33.3 0.3 collective-permute-start.5
  33.6 0.0 collective-permute-done.2.w_1
  33.6 0.2 collective-permute-start.6
  33.8 1.0 %collective-permute-done.3.w_2 = bf16[256,256]{1,0:T(8,128)(2,1)S(1)} collective-permute-done((bf16[256,256]{1,0:T(8,128)(2,1)S(1)}, bf16[256,256]{1,0:T(8,128)(2,1)S(1)}, u32[]{:S(2)}, u32[]{:S(2)}) %collective-permute-start.3) | collective-permute-done | bytes 131104 | tf_op jit(solution)/shard_map/ppermute | solution.py:251
  34.8 1.3 %collective-permute-start.7 = (bf16[256,256]{1,0:T(8,128)(2,1)S(1)}, bf16[256,256]{1,0:T(8,128)(2,1)S(1)}, u32[]{:S(2)}, u32[]{:S(2)}) collective-permute-start(bf16[256,256]{1,0:T(8,128)(2,1)S(1)} %collective-permute-done.3.w_2), channel_id=1, source_target_pairs={{0,1},{1,0},{2,3},{3,2},{4,5},{5,4},{6,7},{7,6},{8,9},{9,8},{10,11... | collective-permute-start | bytes 393224 | tf_op jit(solution)/shard_map/ppermute | solution.py:253
  36.1 0.0 collective-permute-done.4.w_3
  36.1 0.0 collective-permute-start.8
  36.1 0.0 collective-permute-done.t_oth
  36.1 1.0 %own_columns.1 = (bf16[16,96,256]{2,1,0:T(8,128)(2,1)S(1)}, f32[16,96,256]{2,1,0:T(8,128)S(1)}, f32[48,256]{1,0:T(8,128)S(1)}, bf16[4,2,4,32,256]{4,3,2,1,0:T(8,128)(2,1)S(1)}) custom-call(bf16[1536,256]{1,0:T(8,128)(2,1)S(1)} %get-tuple-element.16.t_own, bf16[3072,256]{1,0:T(8,128)(2,1)S(1)} %collective-permute-done.t_oth, ...), custom_call_target="tpu_custom_call" | custom-call | flops 402653184 | bytes 4194304 | tf_op jit(solution)/shard_map/own_columns/pallas_call | solution.py:270
  37.1 0.0 collective-permute-done.5.w_0
  37.1 0.0 collective-permute-done.6.w_1
  37.1 0.0 collective-permute-done.7.w_2
  37.1 0.3 collective-permute-done.8.w_3
  37.4 2.3 %rest.1 = (f32[1,32]{1,0:T(1,128)S(1)}, f32[16,96]{1,0:T(8,128)S(1)}, f32[16,128]{1,0:T(8,128)}) custom-call(bf16[1536,256]{1,0:T(8,128)(2,1)S(1)} %get-tuple-element.16.t_own, bf16[3072,256]{1,0:T(8,128)(2,1)S(1)} %collective-permute-done.t_oth, bf16[16,96,256]{2,1,0:T(8,128)(2,1)S(1)} %get-tuple-element.19.t2_own, ...), custom_call_target="tpu_custom_call" | custom-call | flops 1207959552 | bytes 4194304 | tf_op jit(solution)/shard_map/rest/pallas_call | solution.py:284
  39.7 3.4 %all-to-all-start.1 = ((f32[16,1,128]{2,1,0:T(1,128)}), f32[16,1,128]{2,1,0:T(1,128)S(1)}, u32[]{:S(2)}, u32[]{:S(2)}) async-start(f32[16,1,128]{2,1,0:T(1,128)} %bitcast.5), calls=%async_computation.1 | async-start | bytes 16384 | tf_op jit(solution)/shard_map/all_to_all | solution.py:305
  43.2 0.3 collective-permute-start.9
  43.5 6.7 %all-to-all-done.1 = f32[16,1,128]{2,1,0:T(1,128)S(1)} async-done(((f32[16,1,128]{2,1,0:T(1,128)}), f32[16,1,128]{2,1,0:T(1,128)S(1)}, u32[]{:S(2)}, u32[]{:S(2)}) %all-to-all-start.1) | async-done | bytes 8224 | tf_op jit(solution)/shard_map/all_to_all | solution.py:305
  50.2 0.0 collective-permute-done.9.g_oth
  50.2 0.6 %join.1 = (f32[1,32]{1,0:T(1,128)}, f32[32,96]{1,0:T(8,128)}, f32[1,32]{1,0:T(1,128)}) custom-call(f32[1,128]{1,0:T(1,128)S(1)} %bitcast.10, f32[16,96]{1,0:T(8,128)S(1)} %get-tuple-element.24.grad, f32[16,96]{1,0:T(8,128)S(1)} %collective-permute-done.9.g_oth, f32[1,32]{1,0:T(1,128)S(1)} %get-tuple-element.25.amp), custom_call_target="tpu_custom_call" | custom-call | tf_op jit(solution)/shard_map/join/pallas_call | solution.py:307
  (1 shorter events, 0.0 us)
Async XLA Ops:
  0.6 35.4 %collective-permute-start = (bf16[3072,256]{1,0:T(8,128)(2,1)}, bf16[3072,256]{1,0:T(8,128)(2,1)S(1)}, u32[]{:S(2)}, u32[]{:S(2)}) collective-permute-start(bf16[3072,256]{1,0:T(8,128)(2,1)} %bitcast.11), channel_id=1, source_target_pairs={{0,1},{1,0},{2,3},{3,2},{4,5},{5,4},{6,7},{7,6},{8,9},{9,8},{10,11... | collective-permute-start | bytes 4718600 | tf_op jit(solution)/shard_map/ppermute | solution.py:239
  24.8 8.8 %collective-permute-start.2 = (bf16[256,256]{1,0:T(8,128)(2,1)S(1)}, bf16[256,256]{1,0:T(8,128)(2,1)S(1)}, u32[]{:S(2)}, u32[]{:S(2)}) collective-permute-start(bf16[256,256]{1,0:T(8,128)(2,1)S(1)} %block.1.w_0), channel_id=1, source_target_pairs={{0,16},{16,32},{32,48},{48,0},{1,17},{17,33},{33,49},{49,1},{2,18}... | collective-permute-start | bytes 393224 | tf_op jit(solution)/shard_map/ppermute | solution.py:251
  26.2 8.6 %collective-permute-start.3 = (bf16[256,256]{1,0:T(8,128)(2,1)S(1)}, bf16[256,256]{1,0:T(8,128)(2,1)S(1)}, u32[]{:S(2)}, u32[]{:S(2)}) collective-permute-start(bf16[256,256]{1,0:T(8,128)(2,1)S(1)} %block.1.w_0), channel_id=1, source_target_pairs={{0,32},{16,48},{32,0},{48,16},{1,33},{17,49},{33,1},{49,17},{2,34}... | collective-permute-start | bytes 393224 | tf_op jit(solution)/shard_map/ppermute | solution.py:251
  28.8 7.3 %collective-permute-start.4 = (bf16[256,256]{1,0:T(8,128)(2,1)S(1)}, bf16[256,256]{1,0:T(8,128)(2,1)S(1)}, u32[]{:S(2)}, u32[]{:S(2)}) collective-permute-start(bf16[256,256]{1,0:T(8,128)(2,1)S(1)} %block.1.w_0), channel_id=1, source_target_pairs={{0,48},{16,0},{32,16},{48,32},{1,49},{17,1},{33,17},{49,33},{2,50}... | collective-permute-start | bytes 393224 | tf_op jit(solution)/shard_map/ppermute | solution.py:251
  31.1 2.2 %collective-permute-start.1 = (bf16[64,256]{1,0:T(8,128)(2,1)S(1)}, bf16[64,256]{1,0:T(8,128)(2,1)S(1)}, u32[]{:S(2)}, u32[]{:S(2)}) collective-permute-start(bf16[64,256]{1,0:T(8,128)(2,1)S(1)} %get-tuple-element.17.vl_own), channel_id=1, source_target_pairs={{0,1},{1,0},{2,3},{3,2},{4,5},{5,4},{6,7},{7,6},{8,9},{9,8},{10,11... | collective-permute-start | bytes 98312 | tf_op jit(solution)/shard_map/ppermute | solution.py:269
  33.3 3.8 %collective-permute-start.5 = (bf16[256,256]{1,0:T(8,128)(2,1)S(1)}, bf16[256,256]{1,0:T(8,128)(2,1)S(1)}, u32[]{:S(2)}, u32[]{:S(2)}) collective-permute-start(bf16[256,256]{1,0:T(8,128)(2,1)S(1)} %block.1.w_0), channel_id=1, source_target_pairs={{0,1},{1,0},{2,3},{3,2},{4,5},{5,4},{6,7},{7,6},{8,9},{9,8},{10,11... | collective-permute-start | bytes 393224 | tf_op jit(solution)/shard_map/ppermute | solution.py:253
  33.6 3.5 %collective-permute-start.6 = (bf16[256,256]{1,0:T(8,128)(2,1)S(1)}, bf16[256,256]{1,0:T(8,128)(2,1)S(1)}, u32[]{:S(2)}, u32[]{:S(2)}) collective-permute-start(bf16[256,256]{1,0:T(8,128)(2,1)S(1)} %collective-permute-done.2.w_1), channel_id=1, source_target_pairs={{0,1},{1,0},{2,3},{3,2},{4,5},{5,4},{6,7},{7,6},{8,9},{9,8},{10,11... | collective-permute-start | bytes 393224 | tf_op jit(solution)/shard_map/ppermute | solution.py:253
  34.8 2.3 %collective-permute-start.7 = (bf16[256,256]{1,0:T(8,128)(2,1)S(1)}, bf16[256,256]{1,0:T(8,128)(2,1)S(1)}, u32[]{:S(2)}, u32[]{:S(2)}) collective-permute-start(bf16[256,256]{1,0:T(8,128)(2,1)S(1)} %collective-permute-done.3.w_2), channel_id=1, source_target_pairs={{0,1},{1,0},{2,3},{3,2},{4,5},{5,4},{6,7},{7,6},{8,9},{9,8},{10,11... | collective-permute-start | bytes 393224 | tf_op jit(solution)/shard_map/ppermute | solution.py:253
  36.1 1.3 %collective-permute-start.8 = (bf16[256,256]{1,0:T(8,128)(2,1)S(1)}, bf16[256,256]{1,0:T(8,128)(2,1)S(1)}, u32[]{:S(2)}, u32[]{:S(2)}) collective-permute-start(bf16[256,256]{1,0:T(8,128)(2,1)S(1)} %collective-permute-done.4.w_3), channel_id=1, source_target_pairs={{0,1},{1,0},{2,3},{3,2},{4,5},{5,4},{6,7},{7,6},{8,9},{9,8},{10,11... | collective-permute-start | bytes 393224 | tf_op jit(solution)/shard_map/ppermute | solution.py:253
  39.7 10.5 %all-to-all-start.1 = ((f32[16,1,128]{2,1,0:T(1,128)}), f32[16,1,128]{2,1,0:T(1,128)S(1)}, u32[]{:S(2)}, u32[]{:S(2)}) async-start(f32[16,1,128]{2,1,0:T(1,128)} %bitcast.5), calls=%async_computation.1 | async-start | bytes 16384 | tf_op jit(solution)/shard_map/all_to_all | solution.py:305
  43.2 7.0 %collective-permute-start.9 = (f32[16,96]{1,0:T(8,128)S(1)}, f32[16,96]{1,0:T(8,128)S(1)}, u32[]{:S(2)}, u32[]{:S(2)}) collective-permute-start(f32[16,96]{1,0:T(8,128)S(1)} %get-tuple-element.24.grad), channel_id=1, source_target_pairs={{0,1},{1,0},{2,3},{3,2},{4,5},{5,4},{6,7},{7,6},{8,9},{9,8},{10,11... | collective-permute-start | bytes 18440 | tf_op jit(solution)/shard_map/ppermute | solution.py:304
